TPU v7x, 32 devices: a whole 2x2x4 slice. The times are simulated.
32 devices in a mesh: ctx: 2 (over y), fsdp: 16 (over z, x, core).
Axes of the slice: x: 2, y: 2, z: 4, core: 2. Of those that a mesh axis runs over, the one named last changes fastest.
Arguments:
- tokens: bfloat16 [16, 1024, 768], P('fsdp', 'ctx'), may hold values from -6 to 6
- step_embed: bfloat16 [16, 768], P('fsdp'), may hold values from -3 to 3
- block_ids: int32 [16, 4], P('fsdp', 'ctx'), may hold values from 0 to 3, as said below
- cotangent: bfloat16 [16, 1024, 768], P('fsdp', 'ctx'), may hold values from -6 to 6
- project_weight: float32 [768, 2304], P('fsdp'), may hold values from -0.21875 to 0.21875
- project_bias: float32 [2, 768], P(None, 'fsdp'), may hold values from -2 to 2
- output_weight: float32 [768, 768], P('fsdp'), may hold values from -3 to 3
- output_bias: float32 [768], P('fsdp'), may hold values from -2 to 2
- first_gain: float32 [768], P('fsdp'), may hold values from 0.25 to 1.75
- first_shift: float32 [768], P('fsdp'), may hold values from -2 to 2
- up_weight: float32 [768, 3072], P('fsdp'), may hold values from -0.21875 to 0.21875
- up_bias: float32 [3072], P('fsdp'), may hold values from -3 to 3
- down_weight: float32 [3072, 768], P('fsdp'), may hold values from -0.109375 to 0.109375
- down_bias: float32 [768], P('fsdp'), may hold values from -2 to 2
- second_gain: float32 [768], P('fsdp'), may hold values from 0.25 to 1.75
- second_shift: float32 [768], P('fsdp'), may hold values from -2 to 2
Outputs:
- output: float32 [16, 1024, 768], P('fsdp', 'ctx')
- token_grad: float32 [16, 1024, 768], P('fsdp', 'ctx')
- grad_project_weight: float32 [768, 2304], P('fsdp')
- grad_project_bias: float32 [2, 768], P(None, 'fsdp')
- grad_output_weight: float32 [768, 768], P('fsdp')
- grad_output_bias: float32 [768], P('fsdp')
- grad_first_gain: float32 [768], P('fsdp')
- grad_first_shift: float32 [768], P('fsdp')
- grad_up_weight: float32 [768, 3072], P('fsdp')
- grad_up_bias: float32 [3072], P('fsdp')
- grad_down_weight: float32 [3072, 768], P('fsdp')
- grad_down_bias: float32 [768], P('fsdp')
- grad_second_gain: float32 [768], P('fsdp')
- grad_second_shift: float32 [768], P('fsdp')
Inputs may be any that keep to these rules, and one draw needn't show every extreme that they name: `block_ids`: in every sequence each id appears once, and the two blocks stored on one index of ctx have ids adding to 3.
All inputs are finite; a program needn't handle non-finite values.
Results may differ from a plain program's by a relative error of at most 0.019.
The roundings to bfloat16 on the way count: a program that leaves them out, or rounds other values in their place, can miss the bound.
Values may be sent and summed in bfloat16 or wider, within the bound.
No kernel may reach another device: no remote copies, remote signals or barrier semaphores. Data moves between devices by JAX's collectives and lax.ppermute only.
A program may use at most 192 MiB of HBM per device.

v0:
```python
import functools

import jax
import jax.numpy as jnp
from jax import lax
from jax.experimental import pallas as pl
from jax.experimental.pallas import tpu as pltpu
from jax.sharding import PartitionSpec as P

HEADS = 12


norm_epsilon = 1e-05
masked_score = -1e30


def layer_norm(values, gain, shift):
    center = values - jnp.mean(values, axis=-1, keepdims=True)
    spread = jnp.mean(center * center, axis=-1, keepdims=True)
    return center * lax.rsqrt(spread + norm_epsilon) * gain + shift


def gelu_exact(values):
    return jax.nn.gelu(values, approximate=False)


def product(left, right):
    return jnp.dot(left, right, preferred_element_type=jnp.float32)


def transpose_left(left, right):
    return lax.dot_general(
        left, right, (((0,), (0,)), ((), ())), preferred_element_type=jnp.float32
    )


def transpose_right(left, right):
    return lax.dot_general(
        left, right, (((1,), (1,)), ((), ())), preferred_element_type=jnp.float32
    )


def column_sum(values):
    return jnp.sum(values.astype(jnp.float32), axis=0)


def shards(
    tokens,
    step_embed,
    block_ids,
    cotangent,
    project_weight,
    project_bias,
    output_weight,
    output_bias,
    first_gain,
    first_shift,
    up_weight,
    up_bias,
    down_weight,
    down_bias,
    second_gain,
    second_shift,
):
    gathered = (
        lax.all_gather(project_weight.astype(jnp.bfloat16), "fsdp", axis=0, tiled=True),
        lax.all_gather(project_bias.astype(jnp.bfloat16), "fsdp", axis=1, tiled=True),
        lax.all_gather(output_weight.astype(jnp.bfloat16), "fsdp", axis=0, tiled=True),
        lax.all_gather(output_bias.astype(jnp.bfloat16), "fsdp", axis=0, tiled=True),
        lax.all_gather(first_gain.astype(jnp.bfloat16), "fsdp", axis=0, tiled=True),
        lax.all_gather(first_shift.astype(jnp.bfloat16), "fsdp", axis=0, tiled=True),
        lax.all_gather(up_weight.astype(jnp.bfloat16), "fsdp", axis=0, tiled=True),
        lax.all_gather(up_bias.astype(jnp.bfloat16), "fsdp", axis=0, tiled=True),
        lax.all_gather(down_weight.astype(jnp.bfloat16), "fsdp", axis=0, tiled=True),
        lax.all_gather(down_bias.astype(jnp.bfloat16), "fsdp", axis=0, tiled=True),
        lax.all_gather(second_gain.astype(jnp.bfloat16), "fsdp", axis=0, tiled=True),
        lax.all_gather(second_shift.astype(jnp.bfloat16), "fsdp", axis=0, tiled=True),
    )
    (
        project_matrix,
        project_offset,
        output_matrix,
        output_offset,
        first_scale,
        first_offset,
        up_matrix,
        up_offset,
        down_matrix,
        down_offset,
        second_scale,
        second_offset,
    ) = gathered
    seq_count, pair_rows, width = tokens.shape
    head_dim = width // HEADS
    pair_width = 2 * head_dim
    pair_count = HEADS // 2
    scale = head_dim ** (-0.5)
    flat_rows = seq_count * pair_rows
    pair_indices = jnp.arange(pair_count, dtype=jnp.int32)

    def head_pair(source, pair_index):
        piece = lax.dynamic_slice_in_dim(source, pair_index * pair_width, pair_width, 2)
        return piece.reshape(seq_count, source.shape[1], 2, head_dim)

    def merge_pairs(stacked):
        return jnp.transpose(stacked, (1, 2, 0, 3)).reshape(flat_rows, width)

    hidden_zero = (tokens.astype(jnp.float32) + step_embed.astype(jnp.float32)[:, None, :]).reshape(
        flat_rows, width
    )
    hidden_zero_low = hidden_zero.astype(jnp.bfloat16)
    offsets = project_offset.astype(jnp.float32)
    bias_row = jnp.concatenate([offsets[0], jnp.zeros_like(offsets[0]), offsets[1]])
    projected = (product(hidden_zero_low, project_matrix) + bias_row).astype(jnp.bfloat16)
    queries = projected[:, :width].reshape(seq_count, pair_rows, width)
    keys_here = projected[:, width : 2 * width].reshape(seq_count, pair_rows, width)
    values_here = projected[:, 2 * width :].reshape(seq_count, pair_rows, width)
    keys_all, values_all, ids_all = (
        lax.all_gather(keys_here, "ctx", axis=1, tiled=True),
        lax.all_gather(values_here, "ctx", axis=1, tiled=True),
        lax.all_gather(block_ids.astype(jnp.bfloat16), "ctx", axis=1, tiled=True),
    )
    block_rows = pair_rows // block_ids.shape[1]
    query_ids = jnp.repeat(block_ids, block_rows, axis=1)
    key_ids = jnp.repeat(ids_all.astype(jnp.int32), block_rows, axis=1)
    allowed = key_ids[:, None, None, :] <= query_ids[:, None, :, None]

    def forward_pair(pair_index):
        query_pair = head_pair(queries, pair_index)
        key_pair = head_pair(keys_all, pair_index)
        value_pair = head_pair(values_all, pair_index)
        scores = (
            jnp.einsum("bqhd,bkhd->bhqk", query_pair, key_pair, preferred_element_type=jnp.float32)
            * scale
        )
        scores = jnp.where(allowed, scores, masked_score)
        peak = jnp.max(scores, axis=-1, keepdims=True)
        expon = jnp.exp(scores - peak)
        totals = jnp.sum(expon, axis=-1, keepdims=True)
        probs = expon / totals
        mixed_pair = jnp.einsum(
            "bhqk,bkhd->bqhd",
            probs.astype(jnp.bfloat16),
            value_pair,
            preferred_element_type=jnp.float32,
        )
        log_total = (peak + jnp.log(totals))[..., 0]
        return (
            mixed_pair.astype(jnp.bfloat16).reshape(seq_count, pair_rows, pair_width),
            log_total,
        )

    mixed_pairs, log_totals = lax.map(forward_pair, pair_indices)
    mixed = merge_pairs(mixed_pairs)
    branch = product(mixed, output_matrix) + output_offset.astype(jnp.float32)
    hidden_one, first_pull = jax.vjp(
        layer_norm,
        hidden_zero + branch,
        first_scale.astype(jnp.float32),
        first_offset.astype(jnp.float32),
    )
    hidden_one_low = hidden_one.astype(jnp.bfloat16)
    inner = product(hidden_one_low, up_matrix) + up_offset.astype(jnp.float32)
    activated, gelu_pull = jax.vjp(gelu_exact, inner)
    activated_low = activated.astype(jnp.bfloat16)
    feed = product(activated_low, down_matrix) + down_offset.astype(jnp.float32)
    result, second_pull = jax.vjp(
        layer_norm,
        hidden_one + feed,
        second_scale.astype(jnp.float32),
        second_offset.astype(jnp.float32),
    )
    project_back, output_back, up_back, down_back = (
        lax.all_gather(project_weight.astype(jnp.bfloat16), "fsdp", axis=0, tiled=True),
        lax.all_gather(output_weight.astype(jnp.bfloat16), "fsdp", axis=0, tiled=True),
        lax.all_gather(up_weight.astype(jnp.bfloat16), "fsdp", axis=0, tiled=True),
        lax.all_gather(down_weight.astype(jnp.bfloat16), "fsdp", axis=0, tiled=True),
    )
    grad_second_in, grad_second_gain, grad_second_shift = second_pull(
        cotangent.reshape(flat_rows, width).astype(jnp.float32)
    )
    feed_grad = grad_second_in.astype(jnp.bfloat16)
    grad_down_bias = column_sum(feed_grad)
    grad_down_weight = transpose_left(activated_low, feed_grad)
    activated_grad = transpose_right(feed_grad, down_back)
    inner_grad = gelu_pull(activated_grad)[0].astype(jnp.bfloat16)
    grad_up_bias = column_sum(inner_grad)
    grad_up_weight = transpose_left(hidden_one_low, inner_grad)
    hidden_one_grad = grad_second_in + transpose_right(inner_grad, up_back)
    grad_first_in, grad_first_gain, grad_first_shift = first_pull(hidden_one_grad)
    branch_grad = grad_first_in.astype(jnp.bfloat16)
    grad_output_bias = column_sum(branch_grad)
    grad_output_weight = transpose_left(mixed, branch_grad)
    mixed_grad = (
        transpose_right(branch_grad, output_back)
        .astype(jnp.bfloat16)
        .reshape(seq_count, pair_rows, width)
    )

    def backward_pair(pair_inputs):
        pair_index, log_total = pair_inputs
        query_pair = head_pair(queries, pair_index)
        key_pair = head_pair(keys_all, pair_index)
        value_pair = head_pair(values_all, pair_index)
        grad_pair = head_pair(mixed_grad, pair_index)
        scores = (
            jnp.einsum("bqhd,bkhd->bhqk", query_pair, key_pair, preferred_element_type=jnp.float32)
            * scale
        )
        probs = jnp.where(allowed, jnp.exp(scores - log_total[..., None]), 0.0)
        prob_grad = jnp.einsum(
            "bqhd,bkhd->bhqk", grad_pair, value_pair, preferred_element_type=jnp.float32
        )
        row_dot = jnp.sum(probs * prob_grad, axis=-1, keepdims=True)
        score_grad = (probs * (prob_grad - row_dot)).astype(jnp.bfloat16)
        query_grad = (
            jnp.einsum("bhqk,bkhd->bqhd", score_grad, key_pair, preferred_element_type=jnp.float32)
            * scale
        )
        key_grad = (
            jnp.einsum(
                "bhqk,bqhd->bkhd", score_grad, query_pair, preferred_element_type=jnp.float32
            )
            * scale
        )
        value_grad = jnp.einsum(
            "bhqk,bqhd->bkhd",
            probs.astype(jnp.bfloat16),
            grad_pair,
            preferred_element_type=jnp.float32,
        )
        return (
            query_grad.astype(jnp.bfloat16).reshape(seq_count, pair_rows, pair_width),
            key_grad.reshape(seq_count, key_pair.shape[1], pair_width),
            value_grad.reshape(seq_count, key_pair.shape[1], pair_width),
        )

    query_grads, key_partial, value_partial = lax.map(backward_pair, (pair_indices, log_totals))
    key_sums, value_sums = (
        lax.psum_scatter(
            key_partial.astype(jnp.bfloat16), "ctx", scatter_dimension=2, tiled=True
        ).astype(jnp.float32),
        lax.psum_scatter(
            value_partial.astype(jnp.bfloat16), "ctx", scatter_dimension=2, tiled=True
        ).astype(jnp.float32),
    )
    key_grads = key_sums.astype(jnp.bfloat16)
    value_grads = value_sums.astype(jnp.bfloat16)
    project_grad = jnp.concatenate(
        [merge_pairs(query_grads), merge_pairs(key_grads), merge_pairs(value_grads)], axis=1
    )
    grad_project_bias = jnp.stack(
        [column_sum(project_grad[:, :width]), column_sum(project_grad[:, 2 * width :])]
    )
    grad_project_weight = transpose_left(hidden_zero_low, project_grad)
    input_grad = grad_first_in + transpose_right(project_grad, project_back)
    shares = (
        lax.psum_scatter(
            grad_project_weight.astype(jnp.bfloat16), "fsdp", scatter_dimension=0, tiled=True
        ).astype(jnp.float32),
        lax.psum_scatter(
            grad_project_bias.astype(jnp.bfloat16), "fsdp", scatter_dimension=1, tiled=True
        ).astype(jnp.float32),
        lax.psum_scatter(
            grad_output_weight.astype(jnp.bfloat16), "fsdp", scatter_dimension=0, tiled=True
        ).astype(jnp.float32),
        lax.psum_scatter(
            grad_output_bias.astype(jnp.bfloat16), "fsdp", scatter_dimension=0, tiled=True
        ).astype(jnp.float32),
        lax.psum_scatter(
            grad_first_gain.astype(jnp.bfloat16), "fsdp", scatter_dimension=0, tiled=True
        ).astype(jnp.float32),
        lax.psum_scatter(
            grad_first_shift.astype(jnp.bfloat16), "fsdp", scatter_dimension=0, tiled=True
        ).astype(jnp.float32),
        lax.psum_scatter(
            grad_up_weight.astype(jnp.bfloat16), "fsdp", scatter_dimension=0, tiled=True
        ).astype(jnp.float32),
        lax.psum_scatter(
            grad_up_bias.astype(jnp.bfloat16), "fsdp", scatter_dimension=0, tiled=True
        ).astype(jnp.float32),
        lax.psum_scatter(
            grad_down_weight.astype(jnp.bfloat16), "fsdp", scatter_dimension=0, tiled=True
        ).astype(jnp.float32),
        lax.psum_scatter(
            grad_down_bias.astype(jnp.bfloat16), "fsdp", scatter_dimension=0, tiled=True
        ).astype(jnp.float32),
        lax.psum_scatter(
            grad_second_gain.astype(jnp.bfloat16), "fsdp", scatter_dimension=0, tiled=True
        ).astype(jnp.float32),
        lax.psum_scatter(
            grad_second_shift.astype(jnp.bfloat16), "fsdp", scatter_dimension=0, tiled=True
        ).astype(jnp.float32),
    )
    summed = (
        lax.psum(shares[0].astype(jnp.bfloat16), "ctx").astype(jnp.float32),
        lax.psum(shares[1].astype(jnp.bfloat16), "ctx").astype(jnp.float32),
        lax.psum(shares[2].astype(jnp.bfloat16), "ctx").astype(jnp.float32),
        lax.psum(shares[3].astype(jnp.bfloat16), "ctx").astype(jnp.float32),
        lax.psum(shares[4].astype(jnp.bfloat16), "ctx").astype(jnp.float32),
        lax.psum(shares[5].astype(jnp.bfloat16), "ctx").astype(jnp.float32),
        lax.psum(shares[6].astype(jnp.bfloat16), "ctx").astype(jnp.float32),
        lax.psum(shares[7].astype(jnp.bfloat16), "ctx").astype(jnp.float32),
        lax.psum(shares[8].astype(jnp.bfloat16), "ctx").astype(jnp.float32),
        lax.psum(shares[9].astype(jnp.bfloat16), "ctx").astype(jnp.float32),
        lax.psum(shares[10].astype(jnp.bfloat16), "ctx").astype(jnp.float32),
        lax.psum(shares[11].astype(jnp.bfloat16), "ctx").astype(jnp.float32),
    )
    return (
        result.reshape(seq_count, pair_rows, width),
        input_grad.reshape(seq_count, pair_rows, width),
        summed[0],
        summed[1],
        summed[2],
        summed[3],
        summed[4],
        summed[5],
        summed[6],
        summed[7],
        summed[8],
        summed[9],
        summed[10],
        summed[11],
    )


BF = jnp.bfloat16
F32 = jnp.float32
LOG2E = 1.4426950408889634
VMEM_LIMIT = 28 * 1024 * 1024
UNIT = 1.15e9
LIGHT = 0.3
NT = (((1,), (1,)), ((), ()))
TN = (((0,), (0,)), ((), ()))
BLOCK = 256
SOFT = 32
SOFT_BACK = 16
NORM = 128


def nn_dot(left, right):
    return jnp.dot(left, right, preferred_element_type=F32)


def nt_dot(left, right):
    return lax.dot_general(left, right, NT, preferred_element_type=F32)


def tn_dot(left, right):
    return lax.dot_general(left, right, TN, preferred_element_type=F32)


def call(weight, kernel, grid, in_specs, outs, scratch, args, aliases={}):
    return pl.pallas_call(
        kernel,
        grid_spec=pltpu.PrefetchScalarGridSpec(
            num_scalar_prefetch=1,
            grid=grid,
            in_specs=in_specs,
            out_specs=[spec for spec, _, _ in outs],
            scratch_shapes=scratch,
        ),
        out_shape=[jax.ShapeDtypeStruct(shape, dtype) for _, shape, dtype in outs],
        input_output_aliases=aliases,
        compiler_params=pltpu.CompilerParams(vmem_limit_bytes=VMEM_LIMIT),
        cost_estimate=pl.CostEstimate(flops=int(weight * UNIT), bytes_accessed=1, transcendentals=0),
    )(*args)


def tile(shape, index):
    return pl.BlockSpec(shape, lambda i, info: index(i, info))


def fixed(shape):
    return pl.BlockSpec(shape, lambda i, info: (0,) * len(shape), pipeline_mode=pl.Buffered(1))


PIECES, BLOCKS, IDS, SLOTS, CTX, CORE, DOWN, PLACES, ZS = 0, 16, 32, 36, 40, 41, 42, 58, 66
BIAS_Q, BIAS_V, BIAS_O, GAIN_1, SHIFT_1, BIAS_D, GAIN_2, SHIFT_2, BIAS_U = range(9)


def row(ref, at):
    return ref[at : at + 1, :]


def put_rows(info, pieces, target, rows, base=0):
    at = 0
    for piece in pieces:
        for start in range(0, piece.shape[0], rows):
            place = pl.multiple_of(info[base + at] * rows, 16)
            target[pl.ds(place, rows), :] = piece[start : start + rows, :]
            at += 1


def permute_rows(info, base, source, keep, send, lanes, rows):
    for at in range(16):
        target = keep if at < 8 else send
        place = pl.multiple_of(info[base + at] * rows, 16)
        start = at % 8 * rows
        target[start : start + rows, lanes] = source[pl.ds(place, rows), :]


def by_rows(rows, body, chunk):
    def step(at, carry):
        return body(pl.ds(pl.multiple_of(at * chunk, chunk), chunk), carry)

    return functools.partial(lax.fori_loop, 0, rows // chunk, step)


def fold(values):
    total = values[:8]
    for start in range(8, values.shape[0], 8):
        total = total + values[start : start + 8]
    return total


def mean_last(values):
    return jnp.mean(values, axis=-1, keepdims=True)


def two_heads(values, lane):
    zero = jnp.zeros_like(values)
    return jnp.concatenate([jnp.where(lane < 64, values, zero), jnp.where(lane < 64, zero, values)], axis=0)


def attend_call(info, pair, pairs, tokens, pieces, vectors):
    first = vectors is None
    half_rows, width = tokens[0].shape
    half_rows = half_rows if first else half_rows // 2
    length = 2 * half_rows
    piece_rows = pieces[0].shape[0] // 4
    count = len(pieces)
    part = BLOCK
    specs = [fixed(array.shape) for array in tokens]
    specs += [tile((4 * piece_rows, 384), lambda i, info: (0, pair + i)) for _ in pieces]
    args = [*tokens, *pieces]
    if first:
        specs += [
            pl.BlockSpec((4 * piece_rows, 128), lambda i, info: (0, 3 * width // 256), pipeline_mode=pl.Buffered(1))
            for _ in pieces
        ]
        args += pieces
    else:
        specs += [fixed(vectors.shape)]
        args += [vectors]

    def kernel(info, *rest):
        token_refs, rest = rest[: len(tokens)], rest[len(tokens) :]
        piece_refs, rest = rest[:count], rest[count:]
        at_pair = pl.program_id(0)
        if first:
            small_refs, rest = rest[:count], rest[count:]
            qkv_ref, out_own, out_peer, lse_ref, low_ref, vec_ref, weight, stats, mixed, small = rest
            own_ref, peer_ref, step_ref = token_refs

            @pl.when(at_pair == 0)
            def _():
                put_rows(info, small_refs, small, piece_rows)
                vec_ref[...] = small[...].astype(F32).T[:16, :]
                for slot in range(4):
                    source = own_ref if slot < 2 else peer_ref
                    entries = source[slot % 2 * BLOCK : (slot % 2 + 1) * BLOCK, :].astype(F32)
                    rows = pl.ds(pl.multiple_of(info[IDS + slot] * BLOCK, BLOCK), BLOCK)
                    low_ref[rows, :] = (entries + step_ref[...].astype(F32)).astype(BF)
        else:
            vec_ref, qkv_ref, out_own, out_peer, lse_ref, weight, stats, mixed = rest
            low_ref = token_refs[0]
        put_rows(info, piece_refs, weight, piece_rows)
        lanes = pl.ds(pl.multiple_of(info[CTX] * (width // 2) + 128 * (pair + at_pair), 128), 128)
        query_bias = vec_ref[BIAS_Q : BIAS_Q + 1, lanes]
        value_bias = vec_ref[BIAS_V : BIAS_V + 1, lanes]
        for at in range(2):
            rows = slice(half_rows * at, half_rows * (at + 1))
            result = nn_dot(low_ref[rows, :], weight[...])
            qkv_ref[rows, :128] = (result[:, :128] + query_bias).astype(BF) * jnp.asarray(0.125, BF)
            qkv_ref[rows, 128:256] = result[:, 128:256].astype(BF)
            qkv_ref[rows, 256:] = (result[:, 256:] + value_bias).astype(BF)
        lane = lax.broadcasted_iota(jnp.int32, (part, 128), 1)
        for at in range(4):
            extent = BLOCK * (at + 1)
            rows = slice(at * BLOCK, extent)
            query = two_heads(qkv_ref[rows, :128], lane)
            scores = nt_dot(query, qkv_ref[:extent, 128:256])
            peak = jnp.max(scores, axis=-1, keepdims=True)
            expon = jnp.exp2((scores - peak) * LOG2E)
            total = jnp.sum(expon, axis=-1, keepdims=True)
            result = nn_dot(expon.astype(BF), qkv_ref[:extent, 256:]) * (1.0 / total)
            logs = (peak + jnp.log(total)) * LOG2E
            places = pl.ds(pl.multiple_of(info[SLOTS + at] * BLOCK, BLOCK), BLOCK)
            mixed[places, :] = jnp.where(lane < 64, result[:part], result[part:]).astype(BF)
            stats[rows, :] = jnp.where(lane == 0, logs[:part], logs[part:])
        out_own[...] = mixed[:half_rows, :]
        out_peer[...] = mixed[half_rows:, :]
        lse_ref[...] = stats[...].T[:8, :]

    outs = [
        (tile((length, 384), lambda i, info: (0, i)), (length, 384 * pairs), BF),
        (tile((half_rows, 128), lambda i, info: (0, i)), (half_rows, 128 * pairs), BF),
        (tile((half_rows, 128), lambda i, info: (0, i)), (half_rows, 128 * pairs), BF),
        (tile((8, length), lambda i, info: (i, 0)), (8 * pairs, length), F32),
    ]
    scratch = [pltpu.VMEM((width, 384), BF), pltpu.VMEM((length, 128), F32), pltpu.VMEM((length, 128), BF)]
    if first:
        outs += [(fixed((length, width)), (length, width), BF), (fixed((16, width)), (16, width), F32)]
        scratch += [pltpu.VMEM((width, 128), BF)]
    return call(LIGHT, kernel, (pairs,), specs, outs, scratch, (info, *args))


def attend_back_call(info, qkv_early, qkv_late, own_grad, peer_grad, lse_early, lse_late):
    length = qkv_early.shape[0]
    split = qkv_early.shape[1] // 384
    pairs = split + 1
    half_rows = length // 2
    part = BLOCK

    def kernel(info, early_ref, late_ref, own_ref, peer_ref, lse0_ref, lse1_ref, out_ref, sums_ref, *rest):
        grads, dk, dv, qkv_ref, lse_ref = rest
        lane = lax.broadcasted_iota(jnp.int32, (part, 128), 1)
        early = pl.program_id(0) < split
        qkv_ref[...] = jnp.where(early, early_ref[...], late_ref[...])
        lse_ref[...] = jnp.where(early, lse0_ref[...], lse1_ref[...])
        for slot in range(4):
            source = own_ref if slot < 2 else peer_ref
            place = pl.multiple_of(info[IDS + slot] * BLOCK, BLOCK)
            grads[pl.ds(place, BLOCK), :] = source[slot % 2 * BLOCK : (slot % 2 + 1) * BLOCK, :]
        for at in range(3, -1, -1):
            extent = BLOCK * (at + 1)
            rows = slice(at * BLOCK, extent)
            query = two_heads(qkv_ref[rows, :128], lane)
            grad = two_heads(grads[rows, :], lane)
            logs = jnp.concatenate([lse_ref[0:1, rows], lse_ref[1:2, rows]], axis=1)
            probs = jnp.exp2(nt_dot(qkv_ref[:extent, 128:256], query) * LOG2E - logs)
            prob_grad = nt_dot(qkv_ref[:extent, 256:], grad)
            delta = jnp.sum(probs * prob_grad, axis=0, keepdims=True)
            score_grad = (probs * (prob_grad - delta)).astype(BF)
            value_part = nn_dot(probs.astype(BF), grad)
            key_part = nn_dot(score_grad, query)
            if at == 3:
                dv[...] = value_part
                dk[...] = key_part
            else:
                dv[:extent, :] += value_part
                dk[:extent, :] += key_part
            result = tn_dot(qkv_ref[:extent, 128:256], score_grad)
            result = jnp.concatenate([result[:64, :part], result[64:, part:]], axis=0)
            out_ref[rows, :128] = (result.T * 0.125).astype(BF)
        out_ref[:, 128:256] = dk[...].astype(BF)
        out_ref[:, 256:] = dv[...].astype(BF)
        sums_ref[...] = jnp.zeros_like(sums_ref)
        sums_ref[0:1, :] = jnp.sum(out_ref[:, :128].astype(F32), axis=0, keepdims=True)
        sums_ref[1:2, :] = jnp.sum(out_ref[:, 256:].astype(F32), axis=0, keepdims=True)

    return call(
        LIGHT,
        kernel,
        (pairs,),
        [
            tile((length, 384), lambda i, info: (0, jnp.minimum(i, split - 1))),
            fixed((length, 384)),
            tile((half_rows, 128), lambda i, info: (0, i)),
            tile((half_rows, 128), lambda i, info: (0, i)),
            tile((8, length), lambda i, info: (jnp.minimum(i, split - 1), 0)),
            fixed((8, length)),
        ],
        [
            (tile((length, 384), lambda i, info: (0, i)), (length, 384 * pairs), BF),
            (tile((8, 128), lambda i, info: (i, 0)), (8 * pairs, 128), F32),
        ],
        [
            pltpu.VMEM((length, 128), BF),
            pltpu.VMEM((length, 128), F32),
            pltpu.VMEM((length, 128), F32),
            pltpu.VMEM((length, 384), BF),
            pltpu.VMEM((8, length), F32),
        ],
        (info, qkv_early, qkv_late, own_grad, peer_grad, lse_early, lse_late),
    )


TAIL = (
    0.11967499392384373,
    0.1200623431946099,
    0.10393185617157874,
    0.11668075888774873,
    -0.03403495598672794,
    0.18794905931773562,
    -0.1480832678227233,
    0.03381921655662456,
)


def gelu_both(inner):
    scale = 1.0 / (1.0 + 0.3 * jnp.abs(inner))
    bell = jnp.exp2(inner * inner * (-0.5 * LOG2E))
    tail = TAIL[-1]
    for term in TAIL[-2::-1]:
        tail = tail * scale + term
    tail = tail * scale * bell
    below = jnp.where(inner < 0, tail, 1.0 - tail)
    return inner * below, below + (inner * 0.3989422804014327) * bell


def up_call(info, hidden, up_bias, up_pieces, start, carried):
    first = start is not None
    size = 768
    steps = hidden // 2 // size
    skip = 0 if first else steps
    count = len(up_pieces)
    piece_rows = up_pieces[0].shape[0] // 4
    if first:
        own, step, mixed_own, mixed_peer, vectors = start
        rows, width = own.shape
        parts = len(mixed_own)
        args = [own, step, *mixed_own, *mixed_peer, vectors, *up_pieces]
        specs = [fixed(arg.shape) for arg in args[: 3 + 2 * parts]]
        specs += [fixed((4 * piece_rows, width)) for _ in up_pieces]
        aliases = {}
    else:
        args = list(carried)
        rows, width = args[0].shape
        specs = [fixed(args[0].shape)] + [pl.BlockSpec(memory_space=pl.ANY)] * 2
        aliases = {3 + count + at: at for at in range(2)}
    half = width // 2

    def kernel(info, ub_ref, *rest):
        up_refs, rest = rest[:count], rest[count:]
        if first:
            own_ref, step_ref = rest[:2]
            mo_refs, mp_refs = rest[2 : 2 + parts], rest[2 + parts : 2 + 2 * parts]
            vec_ref = rest[2 + 2 * parts]
            out_refs, rest = rest[3 + 2 * parts : 3 + 2 * parts + count], rest[3 + 2 * parts + count :]
            act_ref, slope_ref, norm_ref, root_ref, low_ref, up_weight, out_weight, total = rest

            @pl.when(pl.program_id(0) == 0)
            def _():
                put_rows(info, out_refs, out_weight, piece_rows)
                here = pl.multiple_of(info[CTX] * half, half)
                there = pl.multiple_of((1 - info[CTX]) * half, half)
                mixed = jnp.concatenate([ref[...] for ref in mo_refs], axis=1)
                total[...] = nn_dot(mixed, out_weight[pl.ds(here, half), :])
                mixed = jnp.concatenate([ref[...] for ref in mp_refs], axis=1)
                total[...] += nn_dot(mixed, out_weight[pl.ds(there, half), :])

                def body(at, carry):
                    entries = own_ref[at, :].astype(F32) + step_ref[...].astype(F32)
                    entries = entries + (total[at, :] + row(vec_ref, BIAS_O))
                    center = entries - mean_last(entries)
                    root = lax.rsqrt(mean_last(center * center) + norm_epsilon)
                    norm = center * root
                    norm_ref[at, :] = norm
                    root_ref[at, :] = jnp.broadcast_to(root, (NORM, 128))
                    low_ref[at, :] = (norm * row(vec_ref, GAIN_1) + row(vec_ref, SHIFT_1)).astype(BF)
                    return carry

                by_rows(rows, body, NORM)(0)
        else:
            low_ref, _, _, act_ref, slope_ref, up_weight = rest

        put_rows(info, up_refs, up_weight, piece_rows)

        def gelu_rows(places, carry):
            act, slope = gelu_both(nn_dot(low_ref[places, :], up_weight[...]) + ub_ref[...])
            act_ref[places, :] = act.astype(BF)
            slope_ref[places, :] = slope.astype(BF)
            return carry

        by_rows(rows, gelu_rows, 256)(0)

    outs = [(tile((rows, size), lambda i, info: (0, skip + i)), (rows, hidden), BF)] * 2
    scratch = [pltpu.VMEM((width, size), BF)]
    if first:
        outs += [
            (fixed((rows, width)), (rows, width), F32),
            (fixed((rows, 128)), (rows, 128), F32),
            (fixed((rows, width)), (rows, width), BF),
        ]
        scratch += [pltpu.VMEM((width, width), BF), pltpu.VMEM((rows, width), F32)]
    at_column = 1 if first else 0
    return call(
        LIGHT,
        kernel,
        (steps,),
        [tile((1, size), lambda i, info: (0, skip + i))]
        + [tile((4 * piece_rows, size), lambda i, info: (0, at_column + i)) for _ in up_pieces]
        + specs,
        outs,
        scratch,
        (info, up_bias, *up_pieces, *args),
        aliases,
    )


def down_call(info, act, norm_one, cotangent, vectors, pieces):
    rows, hidden = act.shape
    width = cotangent.shape[1]
    size, part, run = 256, 128, hidden // 8
    norms, grads = rows // part, 8
    count = len(pieces)
    piece_rows = pieces[0].shape[0] // 4

    def kernel(info, vec_ref, act_in, norm_in, cot_in, *rest):
        refs, rest = rest[:count], rest[count:]
        res_out, dz_out, df_out, sums_ref, keep_out, send_out = rest[:6]
        act_ref, weight, norm_ref, cot_ref, feed, res_ref, dz_ref, df_ref, both = rest[6:15]
        in_sems, piece_sems, norm_sems, grad_sems = rest[15:]

        def copy(source, target, sem):
            return pltpu.make_async_copy(source, target, sem)

        loads = [
            copy(act_in, act_ref, in_sems.at[0]),
            copy(norm_in, norm_ref, in_sems.at[1]),
            copy(cot_in, cot_ref, in_sems.at[2]),
        ]
        weights = []
        for at in range(4 * count):
            place = pl.multiple_of(info[DOWN + at] * piece_rows, 16)
            start = at % 4 * piece_rows
            weights.append(
                copy(
                    refs[at // 4].at[start : start + piece_rows, :],
                    weight.at[pl.ds(place, piece_rows), :],
                    piece_sems.at[at],
                )
            )
        loads[0].start()
        for load in weights:
            load.start()
        loads[1].start()
        loads[2].start()
        loads[0].wait()
        for load in weights:
            load.wait()

        def product(at, carry):
            lanes = pl.ds(pl.multiple_of(at * size, size), size)
            feed[:, lanes] = nn_dot(act_ref[...], weight[:, lanes])
            return carry

        lax.fori_loop(0, width // size, product, 0)
        loads[1].wait()
        loads[2].wait()
        stores = []
        sums_ref[...] = jnp.zeros_like(sums_ref)
        for step in range(norms):
            places = slice(step * part, (step + 1) * part)
            entries = feed[places, :] + row(vec_ref, BIAS_D)
            entries = entries + (norm_ref[places, :] * row(vec_ref, GAIN_1) + row(vec_ref, SHIFT_1))
            center = entries - mean_last(entries)
            root = lax.rsqrt(mean_last(center * center) + norm_epsilon)
            norm = center * root
            res_ref[places, :] = norm * row(vec_ref, GAIN_2) + row(vec_ref, SHIFT_2)
            cot = cot_ref[places, :].astype(F32)
            scaled = cot * row(vec_ref, GAIN_2)
            dz = root * (scaled - mean_last(scaled) - norm * mean_last(scaled * norm))
            dz_ref[places, :] = dz
            low = dz.astype(BF)
            df_ref[places, :] = low
            sums_ref[0:1, :] += jnp.sum(low.astype(F32), axis=0, keepdims=True)
            sums_ref[1:2, :] += jnp.sum(cot * norm, axis=0, keepdims=True)
            sums_ref[2:3, :] += jnp.sum(cot, axis=0, keepdims=True)
            pairs = ((res_ref, res_out), (dz_ref, dz_out), (df_ref, df_out))
            for at, (source, target) in enumerate(pairs):
                stores.append(copy(source.at[places, :], target.at[places, :], norm_sems.at[3 * step + at]))
                stores[-1].start()
        core = info[CORE]
        mine = pl.ds(pl.multiple_of(core * piece_rows, 16), piece_rows)
        theirs = pl.ds(pl.multiple_of((1 - core) * piece_rows, 16), piece_rows)

        def send(at):
            place = pl.ds(pl.multiple_of(info[PLACES + at] * piece_rows, 16), piece_rows)
            return (
                copy(both.at[at, mine, :], keep_out.at[place, :], grad_sems.at[2 * at]),
                copy(both.at[at, theirs, :], send_out.at[place, :], grad_sems.at[2 * at + 1]),
            )

        def grad(at, carry):
            lanes = pl.ds(pl.multiple_of(at * run, run), run)
            both[at] = tn_dot(act_ref[:, lanes], df_ref[...]).astype(BF)
            for store in send(at):
                store.start()
            return carry

        lax.fori_loop(0, grads, grad, 0)
        for store in stores + [store for at in range(grads) for store in send(at)]:
            store.wait()

    anywhere = pl.BlockSpec(memory_space=pl.ANY)
    return call(
        LIGHT,
        kernel,
        (1,),
        [fixed(vectors.shape)] + [anywhere] * (3 + count),
        [
            (anywhere, (rows, width), F32),
            (anywhere, (rows, width), F32),
            (anywhere, (rows, width), BF),
            (fixed((8, width)), (8, width), F32),
            (anywhere, (hidden // 2, width), BF),
            (anywhere, (hidden // 2, width), BF),
        ],
        [
            pltpu.VMEM((rows, hidden), BF),
            pltpu.VMEM((hidden, width), BF),
            pltpu.VMEM((rows, width), F32),
            pltpu.VMEM((rows, width), BF),
            pltpu.VMEM((rows, width), F32),
            pltpu.VMEM((rows, width), F32),
            pltpu.VMEM((rows, width), F32),
            pltpu.VMEM((rows, width), BF),
            pltpu.VMEM((grads, run, width), BF),
            pltpu.SemaphoreType.DMA((3,)),
            pltpu.SemaphoreType.DMA((4 * count,)),
            pltpu.SemaphoreType.DMA((3 * norms,)),
            pltpu.SemaphoreType.DMA((2 * grads,)),
        ],
        (info, vectors, act, norm_one, cotangent, *pieces),
    )


def layer_grad_call(
    info, feed_grad, slope, low_one, second_in, norm_one, root_one, vectors, mixed_own, mixed_peer, down, first, second
):
    rows, width = feed_grad.shape
    hidden = slope.shape[1]
    steps = hidden // width
    count = len(down)
    down_rows, up_rows = down[0].shape[0] // 4, first[0].shape[0] // 4
    half = width // 2
    pairs = len(mixed_own)

    def kernel(info, df_ref, slope_ref, low_ref, dz_ref, norm_ref, root_ref, vec_ref, *rest):
        mixed_refs, rest = rest[: 2 * pairs], rest[2 * pairs :]
        down_refs, first_refs, second_refs, out_refs = (rest[count * at : count * at + count] for at in range(4))
        rest = rest[4 * count :]
        keep_ref, send_ref, bias_ref, dz1_ref, own_ref, peer_ref, sums_ref = rest[:7]
        down_weight, up_weight, total, both, da = rest[7:]
        at = pl.program_id(0)

        @pl.when(at == 0)
        def _():
            total[...] = dz_ref[...]

        here_z = info[ZS + jnp.minimum(at, steps - 1)]

        @pl.when(jnp.logical_and(here_z < steps // 2, at < steps))
        def _():
            put_rows(info, first_refs, up_weight, up_rows)

        @pl.when(jnp.logical_and(here_z >= steps // 2, at < steps))
        def _():
            put_rows(info, second_refs, up_weight, up_rows)

        for far in range(2):

            @pl.when(jnp.logical_and(at >= far * 2, at < far * 2 + 2))
            def _():
                for core in range(2):
                    piece = down_refs[2 * core + far]
                    for step in range(2):
                        place = pl.multiple_of(info[DOWN + 8 * core + step] % 4 * down_rows, 16)
                        down_weight[pl.ds(place, down_rows), :] = piece[step * down_rows : (step + 1) * down_rows, :]

        @pl.when(at < steps)
        def _():
            inner = (nt_dot(df_ref[...], down_weight[...]) * slope_ref[...].astype(F32)).astype(BF)
            bias_ref[...] = jnp.sum(inner.astype(F32), axis=0, keepdims=True)
            both[...] = tn_dot(low_ref[...], inner).astype(BF)
            total[...] += nt_dot(inner, up_weight[...])

        @pl.when(at == steps - 1)
        def _():
            put_rows(info, out_refs, up_weight, up_rows)

            def body(at, carry):
                gain_sum, shift_sum, bias_sum = carry
                grad = total[at, :]
                norm = norm_ref[at, :]
                scaled = grad * row(vec_ref, GAIN_1)
                dz = root_ref[at, 0:1] * (scaled - mean_last(scaled) - norm * mean_last(scaled * norm))
                dz1_ref[at, :] = dz
                low = dz.astype(BF)
                da[at, :] = low
                return gain_sum + fold(grad * norm), shift_sum + fold(grad), bias_sum + fold(low.astype(F32))

            zero = jnp.zeros((8, width), F32)
            gain_sum, shift_sum, bias_sum = by_rows(rows, body, NORM)((zero, zero, zero))
            sums_ref[...] = jnp.zeros_like(sums_ref)
            sums_ref[0:1, :] = jnp.sum(bias_sum, axis=0, keepdims=True)
            sums_ref[1:2, :] = jnp.sum(gain_sum, axis=0, keepdims=True)
            sums_ref[2:3, :] = jnp.sum(shift_sum, axis=0, keepdims=True)
            here = pl.multiple_of(info[CTX] * half, half)
            there = pl.multiple_of((1 - info[CTX]) * half, half)
            own_ref[...] = nt_dot(da[...], up_weight[pl.ds(here, half), :]).astype(BF)
            peer_ref[...] = nt_dot(da[...], up_weight[pl.ds(there, half), :]).astype(BF)

        @pl.when(at == steps)
        def _():
            for side, start in ((0, info[CTX] * half), (1, (1 - info[CTX]) * half)):
                mixed = jnp.concatenate([ref[...] for ref in mixed_refs[side * pairs : (side + 1) * pairs]], axis=1)
                both[pl.ds(pl.multiple_of(start, half), half), :] = tn_dot(mixed, da[...]).astype(BF)

        permute_rows(info, BLOCKS, both, keep_ref, send_ref, slice(None), up_rows)

    def step_at(i, info):
        return (0, info[ZS + jnp.minimum(i, steps - 1)])

    def first_at(i, info):
        return (0, 1 + jnp.minimum(info[ZS + jnp.minimum(i, steps - 1)], 1))

    def second_at(i, info):
        return (0, jnp.maximum(info[ZS + jnp.minimum(i, steps - 1)] - 2, 0))

    def grads_at(i, info):
        return (0, jnp.where(i < steps, info[ZS + jnp.minimum(i, steps - 1)], steps))

    columns = hidden + width
    return call(
        LIGHT,
        kernel,
        (steps + 1,),
        [
            fixed((rows, width)),
            tile((rows, width), step_at),
            fixed((rows, width)),
            fixed((rows, width)),
            fixed((rows, width)),
            fixed((rows, 128)),
            fixed(vectors.shape),
        ]
        + [fixed(array.shape) for array in (*mixed_own, *mixed_peer)]
        + [
            tile((2 * down_rows, width), lambda i, info, far=far: (jnp.clip(i - 2 * far, 0, 1), 0))
            for _ in range(2)
            for far in range(2)
        ]
        + [tile((4 * up_rows, width), first_at) for _ in first]
        + [tile((4 * up_rows, width), second_at) for _ in second]
        + [fixed((4 * up_rows, width)) for _ in first],
        [
            (tile((half, width), grads_at), (half, columns), BF),
            (tile((half, width), grads_at), (half, columns), BF),
            (tile((1, width), step_at), (1, hidden), F32),
            (fixed((rows, width)), (rows, width), F32),
            (fixed((rows, half)), (rows, half), BF),
            (fixed((rows, half)), (rows, half), BF),
            (fixed((8, width)), (8, width), F32),
        ],
        [
            pltpu.VMEM((width, width), BF),
            pltpu.VMEM((width, width), BF),
            pltpu.VMEM((rows, width), F32),
            pltpu.VMEM((width, width), BF),
            pltpu.VMEM((rows, width), BF),
        ],
        (
            info,
            feed_grad,
            slope,
            low_one,
            second_in,
            norm_one,
            root_one,
            vectors,
            *mixed_own,
            *mixed_peer,
            *down,
            *first,
            *second,
            *first,
        ),
    )


def project_grad_call(info, low_zero, grads, sums):
    length, width = low_zero.shape
    half = width // 2
    rows = width // 16
    parts = len(sums) - 3
    total = grads.shape[1]

    def kernel(info, low_ref, grad_ref, *rest):
        sum_refs, (keep_ref, send_ref, both, stacked, columns) = rest[: parts + 3], rest[parts + 3 :]
        for start in range(0, total, 384):
            both[...] = tn_dot(low_ref[...], grad_ref[:, start : start + 384]).astype(BF)
            permute_rows(info, BLOCKS, both, keep_ref, send_ref, slice(start, start + 384), rows)
        stacked[...] = jnp.zeros_like(stacked)
        step = 0
        for ref in sum_refs[:parts]:
            for start in range(0, ref.shape[0], 8):
                lanes = pl.ds(pl.multiple_of(info[CTX] * half + 128 * step, 128), 128)
                stacked[0:8, lanes] = ref[start : start + 8, :]
                step += 1
        for step in range(3):
            stacked[8 + 8 * step : 16 + 8 * step, :] = sum_refs[parts + step][...]
        columns[...] = stacked[...].T.astype(BF)
        permute_rows(info, BLOCKS, columns, keep_ref, send_ref, slice(total, total + 128), rows)

    return call(
        LIGHT,
        kernel,
        (1,),
        [fixed((length, width)), fixed(grads.shape)] + [fixed(array.shape) for array in sums],
        [(fixed((half, total + 128)), (half, total + 128), BF)] * 2,
        [pltpu.VMEM((width, 384), BF), pltpu.VMEM((128, width), F32), pltpu.VMEM((width, 128), BF)],
        (info, low_zero, grads, *sums),
    )


def token_grad_call(info, first_slot, grads, pieces, extra):
    rows = pieces[0].shape[0] // 4
    total = grads.shape[1]
    count = len(pieces)
    extras = [] if extra is None else [extra]
    dtype = BF if extra is None else F32
    width = 16 * rows

    def kernel(info, grad_ref, *rest):
        refs, rest = rest[:count], rest[count:]
        extra_refs, (out_ref, weight) = rest[: len(extras)], rest[len(extras) :]
        put_rows(info, refs, weight, rows)
        for step in range(2):
            places = pl.ds(pl.multiple_of(info[IDS + first_slot + step] * BLOCK, BLOCK), BLOCK)
            result = nt_dot(grad_ref[places, :], weight[...])
            target = slice(step * BLOCK, (step + 1) * BLOCK)
            for ref in extra_refs:
                result = result + ref[target, :]
            out_ref[target, :] = result.astype(dtype)

    return call(
        LIGHT,
        kernel,
        (1,),
        [fixed(grads.shape)]
        + [fixed((4 * rows, total)) for _ in pieces]
        + [fixed(array.shape) for array in extras],
        [(fixed((2 * BLOCK, width)), (2 * BLOCK, width), dtype)],
        [pltpu.VMEM((width, total), BF)],
        (info, grads, *pieces, *extras),
    )[0]


def split_heads_shards(
    ring,
    tokens,
    step_embed,
    block_ids,
    cotangent,
    project_weight,
    project_bias,
    output_weight,
    output_bias,
    first_gain,
    first_shift,
    up_weight,
    up_bias,
    down_weight,
    down_bias,
    second_gain,
    second_shift,
):
    rows, width = tokens.shape[1:]
    half = width // 2
    hidden = up_weight.shape[1]
    spot = lax.axis_index("fsdp")
    ctx = lax.axis_index("ctx")
    core = spot % 2

    def flip(array, bit):
        return lax.ppermute(array, "fsdp", [(at, at ^ bit) for at in range(ring)])

    def ctx_flip(array):
        return lax.ppermute(array, "ctx", [(0, 1), (1, 0)])

    def join(array, other):
        return jnp.concatenate([array, other], axis=0)

    def after(values, done):
        return lax.optimization_barrier((values, done))[0]

    def spots(*bits):
        return [spot ^ sum(bit for step, bit in enumerate(bits) if at >> step & 1) for at in range(ring)]

    NEXT, OVER, SIDE = 4, 8, 2
    tokens_own = tokens.reshape(rows, width)
    tokens_peer = ctx_flip(tokens_own)
    ids_peer = ctx_flip(block_ids)
    ids = jnp.concatenate([block_ids, ids_peer], axis=1).reshape(4)
    order = jnp.arange(4, dtype=jnp.int32)
    slots = jnp.sum(jnp.where(ids[None, :] == order[:, None], order[None, :], 0), axis=1)
    z_at, x_at = spot // 4, spot // 2 % 2
    places_of = [(z_at ^ z) % 2 * 4 + (z_at ^ z) // 2 * 2 + (x_at ^ x) for z in range(4) for x in range(2)]
    down_zs = [z_at ^ z for z in (0, 2, 1, 3)]
    info = jnp.concatenate(
        [
            jnp.stack(spots(OVER, NEXT, SIDE, 1) + spots(OVER, NEXT, SIDE, 1)).astype(jnp.int32),
            ids,
            slots,
            jnp.stack([ctx, core] + spots(SIDE, OVER, NEXT, 1) + places_of + down_zs).astype(jnp.int32),
        ]
    )

    pairs = half // 128
    share = width // ring
    hidden_share = hidden // ring
    plane = lax.dynamic_slice_in_dim(project_weight.reshape(share, 3, width), ctx * half, half, 2)
    plane = jnp.transpose(plane.reshape(share, 3, pairs, 128), (0, 2, 1, 3)).reshape(share, 3 * half)
    small = [
        project_bias,
        output_bias[None],
        first_gain[None],
        first_shift[None],
        down_bias[None],
        second_gain[None],
        second_shift[None],
        up_bias.reshape(4, share),
    ]
    small = jnp.concatenate(small, axis=0)
    small = jnp.pad(small, ((0, 128 - small.shape[0]), (0, 0))).T
    project_share = jnp.concatenate([plane, small], axis=1).astype(BF)
    first_share = jnp.concatenate([output_weight, up_weight[:, : hidden // 2]], axis=1).astype(BF)
    second_share = up_weight[:, hidden // 2 :].astype(BF)
    down_share = down_weight.astype(BF)

    project_2 = join(project_share, flip(project_share, OVER))
    down_2 = join(down_share, flip(down_share, SIDE))
    project_4 = join(project_2, flip(project_2, NEXT))
    first_share = after(first_share, project_2)
    first_2 = join(first_share, flip(first_share, OVER))
    project_x = flip(project_4, SIDE)
    second_share = after(second_share, first_2)
    second_got = flip(second_share, OVER)
    first_2 = after(first_2, project_4)
    first_4 = join(first_2, flip(first_2, NEXT))
    project_pieces = [project_4, project_x, *[flip(piece, 1) for piece in (project_4, project_x)]]

    first_x = flip(first_4, SIDE)
    second_2 = after(join(second_share, second_got), first_4)
    second_got = flip(second_2, NEXT)
    down_2 = after(down_2, second_2)
    down_got = flip(down_2, OVER)
    qkv_early, mixed_early, mixed_send, lse_early, low_zero, vectors = attend_call(
        info,
        0,
        pairs - 1,
        [after(tokens_own, (first_4, second_2, down_2)), tokens_peer, step_embed],
        project_pieces,
        None,
    )
    peer_early = ctx_flip(mixed_send)
    up_bias_all = jnp.transpose(vectors[BIAS_U : BIAS_U + 4].reshape(4, ring, share), (1, 0, 2)).reshape(1, hidden)
    second_4 = join(second_2, after(second_got, mixed_send))
    qkv_late, mixed_late, out, lse_late = attend_call(
        info, pairs - 1, 1, [after(low_zero, second_4)], project_pieces, vectors
    )
    mixed_own = [mixed_early, mixed_late]
    mixed_peer = [peer_early, ctx_flip(out)]
    first_x = after(first_x, (out, peer_early))
    second_x = flip(after(second_4, first_x), SIDE)
    down_4 = join(down_2, after(down_got, out))
    down_x = flip(down_4, NEXT)
    first_pieces = [first_4, first_x, *[flip(piece, 1) for piece in (after(first_4, out), first_x)]]
    start = [after(tokens_own, down_4), step_embed, mixed_own, mixed_peer, vectors]
    act, slope, norm_one, root_one, low_one = up_call(info, hidden, up_bias_all, first_pieces, start, None)
    second_pieces = [second_4, second_x, *[flip(piece, 1) for piece in after((second_4, second_x), low_one)]]
    low_next = after(low_one, second_pieces)
    act, slope = up_call(info, hidden, up_bias_all, second_pieces, None, (low_next, act, slope))
    down_pieces = [down_4, down_x, *[flip(piece, 1) for piece in after((down_4, down_x), act)]]
    result, second_in, feed_grad, second_sums, down_keep, down_send = down_call(
        info, act, norm_one, cotangent.reshape(rows, width), vectors, down_pieces
    )

    def add(left, right):
        return (left.astype(F32) + right.astype(F32)).astype(BF)

    def halves(array):
        middle = array.shape[0] // 2
        return array[:middle], array[middle:]

    def add_halves(left, right):
        return [add(*both) for both in zip(halves(left), halves(right))]

    def finish(total):
        return total.astype(F32) + ctx_flip(total).astype(F32)

    down_near, down_far = add_halves(down_keep, flip(down_send, 1))
    feed_next = after(feed_grad, (down_far, down_near))
    down_got = [flip(part, NEXT) for part in halves(down_far)]
    layer_keep, layer_send, up_bias_sums, first_in, grad_own, grad_peer, first_sums = layer_grad_call(
        info,
        feed_next,
        slope,
        low_one,
        second_in,
        norm_one,
        root_one,
        vectors,
        mixed_own,
        mixed_peer,
        down_pieces,
        first_pieces,
        second_pieces,
    )
    grad_recv = ctx_flip(grad_peer)
    down_got = [after(part, layer_keep) for part in down_got]
    layer_got = after(flip(after(layer_send, down_got[0]), 1), grad_recv)
    up_sums = jnp.transpose(up_bias_sums.reshape(ring, 4, share), (1, 0, 2)).reshape(4, width)
    up_sums = jnp.pad(up_sums, ((0, 4), (0, 0)))
    layer_near, layer_far = add_halves(layer_keep, layer_got)
    near_first, near_last = halves(layer_near)
    far_first, far_last = halves(layer_far)
    layer_got_last = flip(far_last, SIDE)
    layer_got_first = flip(far_first, SIDE)
    down_near, down_far = [add(*both) for both in zip(halves(down_near), down_got)]
    down_got = flip(down_far, OVER)
    grad_own = after(grad_own, (layer_far, layer_near, down_far))
    qkv_grads, qkv_sums = attend_back_call(info, qkv_early, qkv_late, grad_own, grad_recv, lse_early, lse_late)
    layer_out = add(near_last, after(layer_got_last, qkv_grads))
    layer_got_last = flip(layer_out, NEXT)
    project_keep, project_send = project_grad_call(
        info, low_zero, after(qkv_grads, layer_out), [qkv_sums, first_sums, second_sums, up_sums]
    )
    peer_part = token_grad_call(info, 2, after(qkv_grads, project_send), project_pieces, None)
    other_part = ctx_flip(peer_part)
    layer_got_first, down_got = after((layer_got_first, down_got), peer_part)
    project_got = flip(after(project_send, (layer_got_first, down_got)), 1)
    project_near, project_far = add_halves(project_keep, after(project_got, peer_part))
    project_got = flip(project_far, SIDE)
    own_part = token_grad_call(info, 0, after(qkv_grads, (project_far, project_near)), project_pieces, first_in)
    layer_near, layer_far = halves(
        after(near_first, own_part).astype(F32) + layer_got_first.astype(F32) + layer_got_last.astype(F32)
    )
    layer_far = layer_far.astype(BF)
    layer_got = flip(layer_far, OVER)
    down_near, down_far = add_halves(down_near, after(down_got, layer_far))
    down_got = flip(down_far, SIDE)
    project_near, project_far = add_halves(project_near, after(project_got, down_far))
    project_got = flip(project_far, NEXT)
    down_total = add(down_near, after(down_got, project_far))
    grad_down_weight = finish(down_total)
    project_near, project_far = add_halves(project_near, after(project_got, down_total))
    layer_total = add(layer_near, after(layer_got, project_far))
    project_half = add(project_near, flip(project_far, OVER))
    token_grad = own_part + after(other_part, project_far).astype(F32)

    layer_sum = finish(layer_total)
    project_other = ctx_flip(project_half)

    def by_kind(array):
        array = array[:, : 3 * half].reshape(share, pairs, 3, 128)
        return jnp.transpose(array, (0, 2, 1, 3)).reshape(share, 3, 1, half)

    mine, other = by_kind(project_half), by_kind(project_other)
    first = ctx == 0
    grad_project_weight = (
        jnp.concatenate([jnp.where(first, mine, other), jnp.where(first, other, mine)], axis=2)
        .reshape(share, 3 * width)
        .astype(F32)
    )
    columns = (project_half[:, 3 * half :].astype(F32) + project_other[:, 3 * half :].astype(F32)).T

    return (
        result.reshape(1, rows, width),
        token_grad.reshape(1, rows, width),
        grad_project_weight,
        columns[:2],
        layer_sum[:, hidden : hidden + width],
        columns[8],
        columns[9],
        columns[10],
        layer_sum[:, :hidden],
        columns[24:28].reshape(hidden_share),
        grad_down_weight,
        columns[16],
        columns[17],
        columns[18],
    )


def solution(mesh):
    ring = mesh.shape["fsdp"]
    body = shards
    if mesh.shape["ctx"] == 2 and ring % 8 == 0 and ring == 16:
        body = functools.partial(split_heads_shards, ring)
    return jax.shard_map(
        body,
        mesh=mesh,
        in_specs=(
            P("fsdp", "ctx", None),
            P("fsdp", None),
            P("fsdp", "ctx"),
            P("fsdp", "ctx", None),
            P("fsdp", None),
            P(None, "fsdp"),
            P("fsdp", None),
            P("fsdp"),
            P("fsdp"),
            P("fsdp"),
            P("fsdp", None),
            P("fsdp"),
            P("fsdp", None),
            P("fsdp"),
            P("fsdp"),
            P("fsdp"),
        ),
        out_specs=(
            P("fsdp", "ctx", None),
            P("fsdp", "ctx", None),
            P("fsdp", None),
            P(None, "fsdp"),
            P("fsdp", None),
            P("fsdp"),
            P("fsdp"),
            P("fsdp"),
            P("fsdp", None),
            P("fsdp"),
            P("fsdp", None),
            P("fsdp"),
            P("fsdp"),
            P("fsdp"),
        ),
        check_vma=False,
    )
```

profile of v0, /device:TPU:0, one launch (start us, length us, event | category | flops | bytes accessed | tf_op | source)
XLA Modules:
  0.0 256.9 jit_solution(12379184953239317429)
XLA Ops:
  0.8 1.2 reshape.130
  2.7 4.1 %collective-permute-start.1 = (bf16[48,1280]{1,0:T(8,128)(2,1)S(1)}, bf16[48,1280]{1,0:T(8,128)(2,1)S(1)}, u32[]{:S(2)}, u32[]{:S(2)}) collective-permute-start(bf16[48,1280]{1,0:T(8,128)(2,1)S(1)} %pad_maximum_fusion.5), channel_id=1, source_target_pairs={{0,8},{1,9},{2,10},{3,11},{4,12},{5,13},{6,14},{7,15},{8,0},{9,1},... | collective-permute-start | bytes 368648 | tf_op jit(solution)/shard_map/ppermute | solution.py:1070
  7.6 1.5 collective-permute-start.6
  9.1 1.5 collective-permute-start
  11.4 1.2 collective-permute-done
  12.8 1.6 collective-permute-start.3
  14.4 2.6 %collective-permute-start.2 = (bf16[48,2304]{1,0:T(8,128)(2,1)S(1)}, bf16[48,2304]{1,0:T(8,128)(2,1)S(1)}, u32[]{:S(2)}, u32[]{:S(2)}) collective-permute-start(bf16[48,2304]{1,0:T(8,128)(2,1)S(1)} %pad_maximum_fusion.4), channel_id=1, source_target_pairs={{0,8},{1,9},{2,10},{3,11},{4,12},{5,13},{6,14},{7,15},{8,0},{9,1},... | collective-permute-start | bytes 663560 | tf_op jit(solution)/shard_map/ppermute | solution.py:1070
  17.0 6.8 %collective-permute-done.2 = bf16[48,2304]{1,0:T(8,128)(2,1)S(1)} collective-permute-done((bf16[48,2304]{1,0:T(8,128)(2,1)S(1)}, bf16[48,2304]{1,0:T(8,128)(2,1)S(1)}, u32[]{:S(2)}, u32[]{:S(2)}) %collective-permute-start.2) | collective-permute-done | bytes 221216 | tf_op jit(solution)/shard_map/ppermute | solution.py:1070
  24.8 3.2 %collective-permute-start.4 = (bf16[96,2304]{1,0:T(8,128)(2,1)S(1)}, bf16[96,2304]{1,0:T(8,128)(2,1)S(1)}, u32[]{:S(2)}, u32[]{:S(2)}) collective-permute-start(bf16[96,2304]{1,0:T(8,128)(2,1)S(1)} %constant_dynamic-update-slice_fusion), channel_id=1, source_target_pairs={{0,4},{1,5},{2,6},{3,7},{4,0},{5,1},{6,2},{7,3},{8,12},{9,13},{10,... | collective-permute-start | bytes 1327112 | tf_op jit(solution)/shard_map/ppermute | solution.py:1070
  28.3 2.3 collective-permute-start.5
  30.6 1.5 collective-permute-start.8
  32.1 8.9 %collective-permute-done.4 = bf16[96,2304]{1,0:T(8,128)(2,1)S(1)} collective-permute-done((bf16[96,2304]{1,0:T(8,128)(2,1)S(1)}, bf16[96,2304]{1,0:T(8,128)(2,1)S(1)}, u32[]{:S(2)}, u32[]{:S(2)}) %collective-permute-start.4) | collective-permute-done | bytes 442400 | tf_op jit(solution)/shard_map/ppermute | solution.py:1070
  41.0 1.6 collective-permute-start.12
  42.9 1.6 collective-permute-start.11
  44.5 1.1 pad_maximum_fusion
  45.6 2.1 collective-permute-start.17
  48.5 10.3 %shard_map.263 = (bf16[1024,768]{1,0:T(8,128)(2,1)S(1)}, bf16[512,256]{1,0:T(8,128)(2,1)S(1)}, bf16[512,256]{1,0:T(8,128)(2,1)S(1)}, f32[16,1024]{1,0:T(8,128)S(...) custom-call(s32[70]{0:T(128)S(1)} %concatenate.47.info, bf16[512,768]{1,0:T(8,128)(2,1)} %bitcast.31.rest_0_.rest_4_, ...), custom_call_target="tpu_custom_call" | custom-call | flops 345000000 | bytes 1 | tf_op jit(solution)/shard_map/pallas_call | solution.py:354
  58.9 1.6 collective-permute-start.13
  61.2 4.8 %shard_map.264 = (bf16[1024,384]{1,0:T(8,128)(2,1)S(1)}, bf16[512,128]{1,0:T(8,128)(2,1)S(1)}, bf16[512,128]{1,0:T(8,128)(2,1)}, f32[8,1024]{1,0:T(8,128)S(1)}) custom-call(s32[70]{0:T(128)S(1)} %concatenate.47.info, bf16[1024,768]{1,0:T(8,128)(2,1)S(1)} %get-tuple-element.97.rest_0_.low_ref, ...), custom_call_target="tpu_custom_call" | custom-call | flops 345000000 | bytes 1 | tf_op jit(solution)/shard_map/pallas_call | solution.py:354
  67.9 6.9 %collective-permute-done.17 = bf16[384,768]{1,0:T(8,128)(2,1)S(1)} collective-permute-done((bf16[384,768]{1,0:T(8,128)(2,1)S(1)}, bf16[384,768]{1,0:T(8,128)(2,1)S(1)}, u32[]{:S(2)}, u32[]{:S(2)}) %collective-permute-start.17) | collective-permute-done | bytes 589856 | tf_op jit(solution)/shard_map/ppermute | solution.py:1070
  76.1 1.5 collective-permute-start.18
  78.4 1.4 copy.110
  83.3 9.1 %shard_map.265 = (bf16[512,3072]{1,0:T(8,128)(2,1)S(1)}, bf16[512,3072]{1,0:T(8,128)(2,1)S(1)}, f32[512,768]{1,0:T(8,128)S(1)}, f32[512,128]{1,0:T(8,128)S(1)}, bf16[512,768]{1,0:T(8,128)(2,1)S(1)}) custom-call(s32[70]{0:T(128)S(1)} %concatenate.47.info, f32[1,3072]{1,0:T(1,128)S(1)} %reshape.135.ub_ref, ...), custom_call_target="tpu_custom_call" | custom-call | flops 345000000 | bytes 1 | tf_op jit(solution)/shard_map/pallas_call | solution.py:354
  93.0 1.8 collective-permute-done.19.rest_2_.rest_14_
  95.3 6.6 %shard_map.266 = (bf16[512,3072]{1,0:T(8,128)(2,1)S(1)}, bf16[512,3072]{1,0:T(8,128)(2,1)S(1)}) custom-call(s32[70]{0:T(128)S(1)} %concatenate.47.info, f32[1,3072]{1,0:T(1,128)S(1)} %reshape.135.ub_ref, bf16[192,1536]{1,0:T(8,128)(2,1)} %constant_dynamic-update-slice_fusion.4.rest_0_.rest_12_, ...), custom_call_target="tpu_custom_call", output_to_operand_aliasing={{0}: (7, {}), {1}: (8, {})} | custom-call | flops 345000000 | bytes 1 | tf_op jit(solution)/shard_map/pallas_call | solution.py:354
  101.9 1.5 collective-permute-done.21.rest_1_.rest_5_
  104.0 2.5 collective-permute-done.22.rest_2_.rest_6_
  106.5 1.7 collective-permute-done.23.rest_3_.rest_7_
  108.2 15.0 %shard_map.267 = (f32[512,768]{1,0:T(8,128)}, f32[512,768]{1,0:T(8,128)S(1)}, bf16[512,768]{1,0:T(8,128)(2,1)S(1)}, f32[8,768]{1,0:T(8,128)S(1)}, bf16[1536,768]...) custom-call(s32[70]{0:T(128)S(1)} %concatenate.47.info, f32[16,768]{1,0:T(8,128)S(1)} %get-tuple-element.93.rest_5_.rest_10_.vec_ref, ...), custom_call_target="tpu_custom_call" | custom-call | flops 345000000 | bytes 1 | tf_op jit(solution)/shard_map/pallas_call | solution.py:354
  123.5 4.4 %collective-permute-done.24 = bf16[1536,768]{1,0:T(8,128)(2,1)S(1)} collective-permute-done((bf16[1536,768]{1,0:T(8,128)(2,1)S(1)}, bf16[1536,768]{1,0:T(8,128)(2,1)S(1)}, u32[]{:S(2)}, u32[]{:S(2)}) %collective-permute-start.24) | collective-permute-done | bytes 2359328 | tf_op jit(solution)/shard_map/ppermute | solution.py:1070
  127.9 1.7 add_convert_fusion.2
  131.0 16.9 %shard_map.268 = (bf16[384,3840]{1,0:T(8,128)(2,1)S(1)}, bf16[384,3840]{1,0:T(8,128)(2,1)S(1)}, f32[1,3072]{1,0:T(1,128)S(1)}, f32[512,768]{1,0:T(8,128)S(1)}, b...) custom-call(s32[70]{0:T(128)S(1)} %concatenate.47.info, ...), custom_call_target="tpu_custom_call" | custom-call | flops 345000000 | bytes 1 | tf_op jit(solution)/shard_map/pallas_call | solution.py:354
  148.0 1.6 collective-permute-start.27
  149.6 1.6 collective-permute-start.28
  151.2 8.4 %collective-permute-done.27.peer_ref = bf16[512,384]{1,0:T(8,128)(2,1)S(1)} collective-permute-done((bf16[512,384]{1,0:T(8,128)(2,1)S(1)}, bf16[512,384]{1,0:T(8,128)(2,1)S(1)}, u32[]{:S(2)}, u32[]{:S(2)}) %collective-permute-start.27) | collective-permute-done | bytes 393248 | tf_op jit(solution)/shard_map/ppermute | solution.py:1073
  159.6 1.8 add_convert_fusion
  161.4 1.3 fusion.1
  162.7 1.5 collective-permute-start.29
  165.7 2.7 %add_convert_fusion.5 = (bf16[384,768]{1,0:T(8,128)(2,1)}, bf16[384,768]{1,0:T(8,128)(2,1)S(1)}) fusion(bf16[384,768]{1,0:T(8,128)(2,1)S(1)} %copy-done.41, bf16[768,768]{1,0:T(8,128)(2,1)} %get-tuple-element.252, bf16[384,768]{1,0:T(8,128)(2,1)} %collective-permute-done.28), kind=kLoop, calls=%fused_computation.7 | loop fusion | flops 2359296 | bytes 3538944 | tf_op jit(solution)/shard_map/convert_element_type | solution.py:1174
  168.4 2.3 collective-permute-start.31
  170.7 1.3 collective-permute-start.30
  172.0 14.5 %shard_map.269 = (bf16[1024,1152]{1,0:T(8,128)(2,1)S(1)}, f32[24,128]{1,0:T(8,128)S(1)}) custom-call(s32[70]{0:T(128)S(1)} %concatenate.47.info, bf16[1024,768]{1,0:T(8,128)(2,1)S(1)} %copy-done.10, bf16[1024,384]{1,0:T(8,128)(2,1)S(1)} %copy-done.23, bf16[512,384]{1,0:T(8,128)(2,1)S(1)} %copy-done.26, bf16[512,384]{1,0:T(8,128)(2,1)S(1)} %copy-done.28, ...), custom_call_target="tpu_custom_call" | custom-call | flops 345000000 | bytes 1 | tf_op jit(solution)/shard_map/pallas_call | solution.py:354
  186.5 2.4 add_convert_fusion.4
  188.9 4.2 %shard_map.270 = (bf16[384,1280]{1,0:T(8,128)(2,1)S(1)}, bf16[384,1280]{1,0:T(8,128)(2,1)}) custom-call(s32[70]{0:T(128)S(1)} %concatenate.47.info, bf16[1024,768]{1,0:T(8,128)(2,1)S(1)} %copy-done.8, bf16[1024,1152]{1,0:T(8,128)(2,1)S(1)} %get-tuple-element.151.grad_ref, f32[24,128]{1,0:T(8,128)S(1)} %get-tuple-element.140.rest_0_, ...), custom_call_target="tpu_custom_call" | custom-call | flops 345000000 | bytes 1 | tf_op jit(solution)/shard_map/pallas_call | solution.py:354
  194.1 2.1 shard_map.271
  198.6 1.2 slice.220
  199.8 1.6 collective-permute-start.33
  201.4 1.6 add_convert_fusion.7
  203.0 1.6 collective-permute-start.34
  204.6 2.1 shard_map.272
  206.7 10.4 %collective-permute-done.35 = bf16[96,3840]{1,0:T(8,128)(2,1)} collective-permute-done((bf16[96,3840]{1,0:T(8,128)(2,1)}, bf16[96,3840]{1,0:T(8,128)(2,1)}, u32[]{:S(2)}, u32[]{:S(2)}) %collective-permute-start.35) | collective-permute-done | bytes 737312 | tf_op jit(solution)/shard_map/ppermute | solution.py:1070
  217.1 1.6 convert_add_fusion
  218.8 1.5 collective-permute-start.40
  220.3 1.6 collective-permute-start.37
  222.5 6.2 %collective-permute-done.37 = bf16[192,768]{1,0:T(8,128)(2,1)S(1)} collective-permute-done((bf16[192,768]{1,0:T(8,128)(2,1)S(1)}, bf16[192,768]{1,0:T(8,128)(2,1)S(1)}, u32[]{:S(2)}, u32[]{:S(2)}) %collective-permute-start.37) | collective-permute-done | bytes 294944 | tf_op jit(solution)/shard_map/ppermute | solution.py:1070
  228.8 1.6 collective-permute-start.42
  230.4 2.9 %collective-permute-done.36 = bf16[96,1280]{1,0:T(8,128)(2,1)S(1)} collective-permute-done((bf16[96,1280]{1,0:T(8,128)(2,1)S(1)}, bf16[96,1280]{1,0:T(8,128)(2,1)S(1)}, u32[]{:S(2)}, u32[]{:S(2)}) %collective-permute-start.36) | collective-permute-done | bytes 245792 | tf_op jit(solution)/shard_map/ppermute | solution.py:1070
  233.3 2.7 %collective-permute-start.38 = (bf16[48,1280]{1,0:T(8,128)(2,1)S(1)}, bf16[48,1280]{1,0:T(8,128)(2,1)S(1)}, u32[]{:S(2)}, u32[]{:S(2)}) collective-permute-start(bf16[48,1280]{1,0:T(8,128)(2,1)S(1)} %add_convert_fusion.16), channel_id=1, source_target_pairs={{0,8},{1,9},{2,10},{3,11},{4,12},{5,13},{6,14},{7,15},{8,0},{9,1},... | collective-permute-start | bytes 368648 | tf_op jit(solution)/shard_map/ppermute | solution.py:1070
  236.0 3.3 %collective-permute-done.40 = bf16[48,3840]{1,0:T(8,128)(2,1)S(1)} collective-permute-done((bf16[48,3840]{1,0:T(8,128)(2,1)S(1)}, bf16[48,3840]{1,0:T(8,128)(2,1)S(1)}, u32[]{:S(2)}, u32[]{:S(2)}) %collective-permute-start.40) | collective-permute-done | bytes 368672 | tf_op jit(solution)/shard_map/ppermute | solution.py:1070
  239.5 1.6 collective-permute-start.41
  241.1 1.3 add_bitcast_fusion
  243.2 1.1 collective-permute-start.39
  245.2 5.8 %collective-permute-done.39 = bf16[48,1280]{1,0:T(8,128)(2,1)S(1)} collective-permute-done((bf16[48,1280]{1,0:T(8,128)(2,1)S(1)}, bf16[48,1280]{1,0:T(8,128)(2,1)S(1)}, u32[]{:S(2)}, u32[]{:S(2)}) %collective-permute-start.39) | collective-permute-done | bytes 122912 | tf_op jit(solution)/shard_map/ppermute | solution.py:1073
  253.2 1.1 reshape.142
  (227 shorter events, 28.2 us)
Async XLA Ops:
  0.7 8.3 %copy-start.55 = (s32[1,2]{1,0:T(1,128)S(1)}, s32[1,2]{1,0:T(1,128)}, u32[]{:S(2)}) copy-start(s32[1,2]{1,0:T(1,128)} %param.18) | copy-start | bytes 28
  0.8 10.4 %copy-start.43 = (f32[48,3072]{1,0:T(8,128)S(1)}, f32[48,3072]{1,0:T(8,128)}, u32[]{:S(2)}) copy-start(f32[48,3072]{1,0:T(8,128)} %param.26) | copy-start | bytes 1769476
  2.2 8.9 %copy-start.46 = (f32[48,768]{1,0:T(8,128)S(1)}, f32[48,768]{1,0:T(8,128)}, u32[]{:S(2)}) copy-start(f32[48,768]{1,0:T(8,128)} %param.22) | copy-start | bytes 442372
  2.7 10.1 %collective-permute-start.1 = (bf16[48,1280]{1,0:T(8,128)(2,1)S(1)}, bf16[48,1280]{1,0:T(8,128)(2,1)S(1)}, u32[]{:S(2)}, u32[]{:S(2)}) collective-permute-start(bf16[48,1280]{1,0:T(8,128)(2,1)S(1)} %pad_maximum_fusion.5), channel_id=1, source_target_pairs={{0,8},{1,9},{2,10},{3,11},{4,12},{5,13},{6,14},{7,15},{8,0},{9,1},... | collective-permute-start | bytes 368648 | tf_op jit(solution)/shard_map/ppermute | solution.py:1070
  7.6 35.3 %collective-permute-start.6 = (bf16[192,768]{1,0:T(8,128)(2,1)}, bf16[192,768]{1,0:T(8,128)(2,1)}, u32[]{:S(2)}, u32[]{:S(2)}) collective-permute-start(bf16[192,768]{1,0:T(8,128)(2,1)} %convert_element_type.206), channel_id=1, source_target_pairs={{0,2},{1,3},{2,0},{3,1},{4,6},{5,7},{6,4},{7,5},{8,10},{9,11},{10,... | collective-permute-start | bytes 884744 | tf_op jit(solution)/shard_map/ppermute | solution.py:1070
  9.1 3.5 %collective-permute-start = (s32[1,2]{1,0:T(1,128)S(1)}, s32[1,2]{1,0:T(1,128)S(1)}, u32[]{:S(2)}, u32[]{:S(2)}) collective-permute-start(s32[1,2]{1,0:T(1,128)S(1)} %copy-done.55), channel_id=1, source_target_pairs={{0,16},{16,0},{1,17},{17,1},{2,18},{18,2},{3,19},{19,3},{4,20},{20... | collective-permute-start | bytes 32 | tf_op jit(solution)/shard_map/ppermute | solution.py:1073
  10.6 35.0 %collective-permute-start.7 = (bf16[512,768]{1,0:T(8,128)(2,1)}, bf16[512,768]{1,0:T(8,128)(2,1)}, u32[]{:S(2)}, u32[]{:S(2)}) collective-permute-start(bf16[512,768]{1,0:T(8,128)(2,1)} %bitcast.31.rest_0_.rest_4_), channel_id=1, source_target_pairs={{0,16},{16,0},{1,17},{17,1},{2,18},{18,2},{3,19},{19,3},{4,20},{20... | collective-permute-start | bytes 2359304 | tf_op jit(solution)/shard_map/ppermute | solution.py:1073
  12.8 11.9 %collective-permute-start.3 = (bf16[96,1280]{1,0:T(8,128)(2,1)S(1)}, bf16[96,1280]{1,0:T(8,128)(2,1)S(1)}, u32[]{:S(2)}, u32[]{:S(2)}) collective-permute-start(bf16[96,1280]{1,0:T(8,128)(2,1)S(1)} %pad_maximum_fusion.3), channel_id=1, source_target_pairs={{0,4},{1,5},{2,6},{3,7},{4,0},{5,1},{6,2},{7,3},{8,12},{9,13},{10,... | collective-permute-start | bytes 737288 | tf_op jit(solution)/shard_map/ppermute | solution.py:1070
  14.4 9.4 %collective-permute-start.2 = (bf16[48,2304]{1,0:T(8,128)(2,1)S(1)}, bf16[48,2304]{1,0:T(8,128)(2,1)S(1)}, u32[]{:S(2)}, u32[]{:S(2)}) collective-permute-start(bf16[48,2304]{1,0:T(8,128)(2,1)S(1)} %pad_maximum_fusion.4), channel_id=1, source_target_pairs={{0,8},{1,9},{2,10},{3,11},{4,12},{5,13},{6,14},{7,15},{8,0},{9,1},... | collective-permute-start | bytes 663560 | tf_op jit(solution)/shard_map/ppermute | solution.py:1070
  24.8 16.2 %collective-permute-start.4 = (bf16[96,2304]{1,0:T(8,128)(2,1)S(1)}, bf16[96,2304]{1,0:T(8,128)(2,1)S(1)}, u32[]{:S(2)}, u32[]{:S(2)}) collective-permute-start(bf16[96,2304]{1,0:T(8,128)(2,1)S(1)} %constant_dynamic-update-slice_fusion), channel_id=1, source_target_pairs={{0,4},{1,5},{2,6},{3,7},{4,0},{5,1},{6,2},{7,3},{8,12},{9,13},{10,... | collective-permute-start | bytes 1327112 | tf_op jit(solution)/shard_map/ppermute | solution.py:1070
  28.3 12.8 %collective-permute-start.5 = (bf16[48,1536]{1,0:T(8,128)(2,1)S(1)}, bf16[48,1536]{1,0:T(8,128)(2,1)S(1)}, u32[]{:S(2)}, u32[]{:S(2)}) collective-permute-start(bf16[48,1536]{1,0:T(8,128)(2,1)S(1)} %get-tuple-element.89), channel_id=1, source_target_pairs={{0,8},{1,9},{2,10},{3,11},{4,12},{5,13},{6,14},{7,15},{8,0},{9,1},... | collective-permute-start | bytes 442376 | tf_op jit(solution)/shard_map/ppermute | solution.py:1070
  30.6 12.0 %collective-permute-start.8 = (bf16[192,1280]{1,0:T(8,128)(2,1)S(1)}, bf16[192,1280]{1,0:T(8,128)(2,1)S(1)}, u32[]{:S(2)}, u32[]{:S(2)}) collective-permute-start(bf16[192,1280]{1,0:T(8,128)(2,1)S(1)} %pad_maximum_fusion.1.rest_3_.rest_7_.rest_1_.rest_0_), channel_id=1, source_target_pairs={{0,2},{1,3},{2,0},{3,1},{4,6},{5,7},{6,4},{7,5},{8,10},{9,11},{10,... | collective-permute-start | bytes 1474568 | tf_op jit(solution)/shard_map/ppermute | solution.py:1070
  32.1 16.4 %copy-start.37 = (bf16[1,768]{1,0:T(2,128)(2,1)S(1)}, bf16[1,768]{1,0:T(2,128)(2,1)}, u32[]{:S(2)}) copy-start(bf16[1,768]{1,0:T(2,128)(2,1)} %rest_5_.1) | copy-start | bytes 4612
  41.0 7.5 %collective-permute-start.9 = (bf16[192,1280]{1,0:T(8,128)(2,1)S(1)}, bf16[192,1280]{1,0:T(8,128)(2,1)S(1)}, u32[]{:S(2)}, u32[]{:S(2)}) collective-permute-start(bf16[192,1280]{1,0:T(8,128)(2,1)S(1)} %pad_maximum_fusion.1.rest_3_.rest_7_.rest_1_.rest_0_), channel_id=1, source_target_pairs={{0,1},{1,0},{2,3},{3,2},{4,5},{5,4},{6,7},{7,6},{8,9},{9,8},{10,11... | collective-permute-start | bytes 1474568 | tf_op jit(solution)/shard_map/ppermute | solution.py:1070
  41.0 25.9 %collective-permute-start.12 = (bf16[192,2304]{1,0:T(8,128)(2,1)S(1)}, bf16[192,2304]{1,0:T(8,128)(2,1)S(1)}, u32[]{:S(2)}, u32[]{:S(2)}) collective-permute-start(bf16[192,2304]{1,0:T(8,128)(2,1)S(1)} %constant_dynamic-update-slice_fusion.2.rest_0_.rest_11_.rest_8_.rest_16_), channel_id=1, source_target_pairs={{0,2},{1,3},{2,0},{3,1},{4,6},{5,7},{6,4},{7,5},{8,10},{9,11},{10,... | collective-permute-start | bytes 2654216 | tf_op jit(solution)/shard_map/ppermute | solution.py:1070
  42.6 5.9 %collective-permute-start.10 = (bf16[192,1280]{1,0:T(8,128)(2,1)S(1)}, bf16[192,1280]{1,0:T(8,128)(2,1)S(1)}, u32[]{:S(2)}, u32[]{:S(2)}) collective-permute-start(bf16[192,1280]{1,0:T(8,128)(2,1)S(1)} %collective-permute-done.8.rest_4_.rest_8_.rest_2_.rest_1_), channel_id=1, source_target_pairs={{0,1},{1,0},{2,3},{3,2},{4,5},{5,4},{6,7},{7,6},{8,9},{9,8},{10,11... | collective-permute-start | bytes 1474568 | tf_op jit(solution)/shard_map/ppermute | solution.py:1070
  42.9 17.6 %collective-permute-start.11 = (bf16[96,1536]{1,0:T(8,128)(2,1)S(1)}, bf16[96,1536]{1,0:T(8,128)(2,1)S(1)}, u32[]{:S(2)}, u32[]{:S(2)}) collective-permute-start(bf16[96,1536]{1,0:T(8,128)(2,1)S(1)} %pad_maximum_fusion.2), channel_id=1, source_target_pairs={{0,4},{1,5},{2,6},{3,7},{4,0},{5,1},{6,2},{7,3},{8,12},{9,13},{10,... | collective-permute-start | bytes 884744 | tf_op jit(solution)/shard_map/ppermute | solution.py:1070
  45.6 29.1 %collective-permute-start.17 = (bf16[384,768]{1,0:T(8,128)(2,1)S(1)}, bf16[384,768]{1,0:T(8,128)(2,1)S(1)}, u32[]{:S(2)}, u32[]{:S(2)}) collective-permute-start(bf16[384,768]{1,0:T(8,128)(2,1)S(1)} %pad_maximum_fusion), channel_id=1, source_target_pairs={{0,8},{1,9},{2,10},{3,11},{4,12},{5,13},{6,14},{7,15},{8,0},{9,1},... | collective-permute-start | bytes 1769480 | tf_op jit(solution)/shard_map/ppermute | solution.py:1070
  48.5 12.7 %copy-start.1 = (bf16[192,1280]{1,0:T(8,128)(2,1)}, bf16[192,1280]{1,0:T(8,128)(2,1)S(1)}, u32[]{:S(2)}) copy-start(bf16[192,1280]{1,0:T(8,128)(2,1)S(1)} %collective-permute-done.9.rest_5_.rest_9_.rest_3_.rest_2_) | copy-start | bytes 1474564
  48.5 12.7 %copy-start.4 = (bf16[192,1280]{1,0:T(8,128)(2,1)}, bf16[192,1280]{1,0:T(8,128)(2,1)S(1)}, u32[]{:S(2)}) copy-start(bf16[192,1280]{1,0:T(8,128)(2,1)S(1)} %collective-permute-done.10.rest_6_.rest_10_.rest_4_.rest_3_) | copy-start | bytes 1474564
  58.9 7.2 %copy-start.7 = (bf16[1024,768]{1,0:T(8,128)(2,1)}, bf16[1024,768]{1,0:T(8,128)(2,1)S(1)}, u32[]{:S(2)}) copy-start(bf16[1024,768]{1,0:T(8,128)(2,1)S(1)} %get-tuple-element.97.rest_0_.low_ref) | copy-start | bytes 4718596
  58.9 7.2 %copy-start.9 = (bf16[1024,768]{1,0:T(8,128)(2,1)}, bf16[1024,768]{1,0:T(8,128)(2,1)S(1)}, u32[]{:S(2)}) copy-start(bf16[1024,768]{1,0:T(8,128)(2,1)S(1)} %get-tuple-element.117.early_ref) | copy-start | bytes 4718596
  58.9 7.2 %copy-start.13 = (bf16[512,256]{1,0:T(8,128)(2,1)}, bf16[512,256]{1,0:T(8,128)(2,1)S(1)}, u32[]{:S(2)}) copy-start(bf16[512,256]{1,0:T(8,128)(2,1)S(1)} %get-tuple-element.104.rest_6_.rest_0_) | copy-start | bytes 786436
  58.9 7.2 %copy-start.29 = (f32[16,1024]{1,0:T(8,128)}, f32[16,1024]{1,0:T(8,128)S(1)}, u32[]{:S(2)}) copy-start(f32[16,1024]{1,0:T(8,128)S(1)} %get-tuple-element.135.lse0_ref) | copy-start | bytes 196612
  58.9 8.0 %collective-permute-start.13 = (bf16[512,256]{1,0:T(8,128)(2,1)S(1)}, bf16[512,256]{1,0:T(8,128)(2,1)S(1)}, u32[]{:S(2)}, u32[]{:S(2)}) collective-permute-start(bf16[512,256]{1,0:T(8,128)(2,1)S(1)} %get-tuple-element.94), channel_id=1, source_target_pairs={{0,16},{16,0},{1,17},{17,1},{2,18},{18,2},{3,19},{19,3},{4,20},{20... | collective-permute-start | bytes 786440 | tf_op jit(solution)/shard_map/ppermute | solution.py:1073
  66.1 8.7 %copy-start.22 = (bf16[1024,384]{1,0:T(8,128)(2,1)}, bf16[1024,384]{1,0:T(8,128)(2,1)S(1)}, u32[]{:S(2)}) copy-start(bf16[1024,384]{1,0:T(8,128)(2,1)S(1)} %get-tuple-element.118.late_ref) | copy-start | bytes 2359300
  66.1 9.2 %copy-start.31 = (f32[8,1024]{1,0:T(8,128)}, f32[8,1024]{1,0:T(8,128)S(1)}, u32[]{:S(2)}) copy-start(f32[8,1024]{1,0:T(8,128)S(1)} %get-tuple-element.136.lse1_ref) | copy-start | bytes 98308
  66.1 15.4 %collective-permute-start.15 = (bf16[192,2304]{1,0:T(8,128)(2,1)S(1)}, bf16[192,2304]{1,0:T(8,128)(2,1)}, u32[]{:S(2)}, u32[]{:S(2)}) collective-permute-start(bf16[192,2304]{1,0:T(8,128)(2,1)S(1)} %constant_dynamic-update-slice_fusion.2.rest_0_.rest_11_.rest_8_.rest_16_), channel_id=1, source_target_pairs={{0,1},{1,0},{2,3},{3,2},{4,5},{5,4},{6,7},{7,6},{8,9},{9,8},{10,11... | collective-permute-start | bytes 2654216 | tf_op jit(solution)/shard_map/ppermute | solution.py:1070
  66.9 14.5 %collective-permute-start.16 = (bf16[192,2304]{1,0:T(8,128)(2,1)S(1)}, bf16[192,2304]{1,0:T(8,128)(2,1)}, u32[]{:S(2)}, u32[]{:S(2)}) collective-permute-start(bf16[192,2304]{1,0:T(8,128)(2,1)S(1)} %collective-permute-done.12.rest_1_.rest_12_.rest_9_.rest_17_), channel_id=1, source_target_pairs={{0,1},{1,0},{2,3},{3,2},{4,5},{5,4},{6,7},{7,6},{8,9},{9,8},{10,11... | collective-permute-start | bytes 2654216 | tf_op jit(solution)/shard_map/ppermute | solution.py:1070
  74.7 17.7 %collective-permute-start.14 = (bf16[192,1536]{1,0:T(8,128)(2,1)}, bf16[192,1536]{1,0:T(8,128)(2,1)S(1)}, u32[]{:S(2)}, u32[]{:S(2)}) collective-permute-start(bf16[192,1536]{1,0:T(8,128)(2,1)} %constant_dynamic-update-slice_fusion.4.rest_0_.rest_12_), channel_id=1, source_target_pairs={{0,2},{1,3},{2,0},{3,1},{4,6},{5,7},{6,4},{7,5},{8,10},{9,11},{10,... | collective-permute-start | bytes 1769480 | tf_op jit(solution)/shard_map/ppermute | solution.py:1070
  76.1 27.3 %collective-permute-start.21 = (bf16[768,768]{1,0:T(8,128)(2,1)}, bf16[768,768]{1,0:T(8,128)(2,1)}, u32[]{:S(2)}, u32[]{:S(2)}) collective-permute-start(bf16[768,768]{1,0:T(8,128)(2,1)} %constant_dynamic-update-slice_fusion.6.rest_0_.rest_4_), channel_id=1, source_target_pairs={{0,4},{1,5},{2,6},{3,7},{4,0},{5,1},{6,2},{7,3},{8,12},{9,13},{10,... | collective-permute-start | bytes 3538952 | tf_op jit(solution)/shard_map/ppermute | solution.py:1070
  76.1 5.3 %collective-permute-start.18 = (bf16[512,128]{1,0:T(8,128)(2,1)}, bf16[512,128]{1,0:T(8,128)(2,1)}, u32[]{:S(2)}, u32[]{:S(2)}) collective-permute-start(bf16[512,128]{1,0:T(8,128)(2,1)} %get-tuple-element.98), channel_id=1, source_target_pairs={{0,16},{16,0},{1,17},{17,1},{2,18},{18,2},{3,19},{19,3},{4,20},{20... | collective-permute-start | bytes 393224 | tf_op jit(solution)/shard_map/ppermute | solution.py:1073
  92.4 2.3 collective-permute-start.19
  92.5 2.8 %collective-permute-start.20 = (bf16[192,1536]{1,0:T(8,128)(2,1)S(1)}, bf16[192,1536]{1,0:T(8,128)(2,1)S(1)}, u32[]{:S(2)}, u32[]{:S(2)}) collective-permute-start(bf16[192,1536]{1,0:T(8,128)(2,1)S(1)} %collective-permute-done.14.rest_1_.rest_13_), channel_id=1, source_target_pairs={{0,1},{1,0},{2,3},{3,2},{4,5},{5,4},{6,7},{7,6},{8,9},{9,8},{10,11... | collective-permute-start | bytes 1769480 | tf_op jit(solution)/shard_map/ppermute | solution.py:1070
  95.3 12.9 %copy-start.21 = (bf16[1,512,768]{2,1,0:T(8,128)(2,1)S(1)}, bf16[1,512,768]{2,1,0:T(8,128)(2,1)}, u32[]{:S(2)}) copy-start(bf16[1,512,768]{2,1,0:T(8,128)(2,1)} %param.19) | copy-start | bytes 2359300
  101.9 21.3 %copy-start = (bf16[512,3072]{1,0:T(8,128)(2,1)}, bf16[512,3072]{1,0:T(8,128)(2,1)S(1)}, u32[]{:S(2)}) copy-start(bf16[512,3072]{1,0:T(8,128)(2,1)S(1)} %get-tuple-element.123.slope_ref) | copy-start | bytes 9437188
  103.5 3.1 %collective-permute-start.22 = (bf16[768,768]{1,0:T(8,128)(2,1)}, bf16[768,768]{1,0:T(8,128)(2,1)S(1)}, u32[]{:S(2)}, u32[]{:S(2)}) collective-permute-start(bf16[768,768]{1,0:T(8,128)(2,1)} %constant_dynamic-update-slice_fusion.6.rest_0_.rest_4_), channel_id=1, source_target_pairs={{0,1},{1,0},{2,3},{3,2},{4,5},{5,4},{6,7},{7,6},{8,9},{9,8},{10,11... | collective-permute-start | bytes 3538952 | tf_op jit(solution)/shard_map/ppermute | solution.py:1070
  103.5 4.7 %collective-permute-start.23 = (bf16[768,768]{1,0:T(8,128)(2,1)}, bf16[768,768]{1,0:T(8,128)(2,1)S(1)}, u32[]{:S(2)}, u32[]{:S(2)}) collective-permute-start(bf16[768,768]{1,0:T(8,128)(2,1)} %collective-permute-done.21.rest_1_.rest_5_), channel_id=1, source_target_pairs={{0,1},{1,0},{2,3},{3,2},{4,5},{5,4},{6,7},{7,6},{8,9},{9,8},{10,11... | collective-permute-start | bytes 3538952 | tf_op jit(solution)/shard_map/ppermute | solution.py:1070
  123.3 4.6 %collective-permute-start.24 = (bf16[1536,768]{1,0:T(8,128)(2,1)S(1)}, bf16[1536,768]{1,0:T(8,128)(2,1)S(1)}, u32[]{:S(2)}, u32[]{:S(2)}) collective-permute-start(bf16[1536,768]{1,0:T(8,128)(2,1)S(1)} %get-tuple-element.121), channel_id=1, source_target_pairs={{0,1},{1,0},{2,3},{3,2},{4,5},{5,4},{6,7},{7,6},{8,9},{9,8},{10,11... | collective-permute-start | bytes 7077896 | tf_op jit(solution)/shard_map/ppermute | solution.py:1070
  130.4 17.5 %collective-permute-start.25 = (bf16[384,768]{1,0:T(8,128)(2,1)S(1)}, bf16[384,768]{1,0:T(8,128)(2,1)S(1)}, u32[]{:S(2)}, u32[]{:S(2)}) collective-permute-start(bf16[384,768]{1,0:T(8,128)(2,1)S(1)} %get-tuple-element.261), channel_id=1, source_target_pairs={{0,4},{1,5},{2,6},{3,7},{4,0},{5,1},{6,2},{7,3},{8,12},{9,13},{10,... | collective-permute-start | bytes 1769480 | tf_op jit(solution)/shard_map/ppermute | solution.py:1070
  147.9 13.5 %copy-start.11 = (f32[512,768]{1,0:T(8,128)}, f32[512,768]{1,0:T(8,128)S(1)}, u32[]{:S(2)}) copy-start(f32[512,768]{1,0:T(8,128)S(1)} %get-tuple-element.152.rest_4_) | copy-start | bytes 4718596
  147.9 13.5 %copy-start.25 = (bf16[512,384]{1,0:T(8,128)(2,1)}, bf16[512,384]{1,0:T(8,128)(2,1)S(1)}, u32[]{:S(2)}) copy-start(bf16[512,384]{1,0:T(8,128)(2,1)S(1)} %get-tuple-element.134.own_ref) | copy-start | bytes 1179652
  147.9 13.5 %copy-start.35 = (f32[8,768]{1,0:T(8,128)}, f32[8,768]{1,0:T(8,128)S(1)}, u32[]{:S(2)}) copy-start(f32[8,768]{1,0:T(8,128)S(1)} %get-tuple-element.141.rest_1_) | copy-start | bytes 73732
  147.9 13.5 %copy-start.40 = (bf16[384,768]{1,0:T(8,128)(2,1)}, bf16[384,768]{1,0:T(8,128)(2,1)S(1)}, u32[]{:S(2)}) copy-start(bf16[384,768]{1,0:T(8,128)(2,1)S(1)} %collective-permute-done.25) | copy-start | bytes 1769476
  147.9 11.6 %collective-permute-start.26 = (bf16[384,3840]{1,0:T(8,128)(2,1)S(1)}, bf16[384,3840]{1,0:T(8,128)(2,1)S(1)}, u32[]{:S(2)}, u32[]{:S(2)}) collective-permute-start(bf16[384,3840]{1,0:T(8,128)(2,1)S(1)} %get-tuple-element.130), channel_id=1, source_target_pairs={{0,1},{1,0},{2,3},{3,2},{4,5},{5,4},{6,7},{7,6},{8,9},{9,8},{10,11... | collective-permute-start | bytes 8847368 | tf_op jit(solution)/shard_map/ppermute | solution.py:1070
  148.0 11.5 %collective-permute-start.27 = (bf16[512,384]{1,0:T(8,128)(2,1)S(1)}, bf16[512,384]{1,0:T(8,128)(2,1)S(1)}, u32[]{:S(2)}, u32[]{:S(2)}) collective-permute-start(bf16[512,384]{1,0:T(8,128)(2,1)S(1)} %get-tuple-element.131), channel_id=1, source_target_pairs={{0,16},{16,0},{1,17},{17,1},{2,18},{18,2},{3,19},{19,3},{4,20},{20... | collective-permute-start | bytes 1179656 | tf_op jit(solution)/shard_map/ppermute | solution.py:1073
  149.6 16.1 %collective-permute-start.28 = (bf16[384,768]{1,0:T(8,128)(2,1)}, bf16[384,768]{1,0:T(8,128)(2,1)}, u32[]{:S(2)}, u32[]{:S(2)}) collective-permute-start(bf16[384,768]{1,0:T(8,128)(2,1)} %get-tuple-element.260), channel_id=1, source_target_pairs={{0,4},{1,5},{2,6},{3,7},{4,0},{5,1},{6,2},{7,3},{8,12},{9,13},{10,... | collective-permute-start | bytes 1769480 | tf_op jit(solution)/shard_map/ppermute | solution.py:1070
  162.7 23.8 %collective-permute-start.29 = (bf16[96,3840]{1,0:T(8,128)(2,1)}, bf16[96,3840]{1,0:T(8,128)(2,1)}, u32[]{:S(2)}, u32[]{:S(2)}) collective-permute-start(bf16[96,3840]{1,0:T(8,128)(2,1)} %get-tuple-element.257), channel_id=1, source_target_pairs={{0,2},{1,3},{2,0},{3,1},{4,6},{5,7},{6,4},{7,5},{8,10},{9,11},{10,... | collective-permute-start | bytes 2211848 | tf_op jit(solution)/shard_map/ppermute | solution.py:1070
  168.4 28.7 %collective-permute-start.31 = (bf16[384,768]{1,0:T(8,128)(2,1)S(1)}, bf16[384,768]{1,0:T(8,128)(2,1)S(1)}, u32[]{:S(2)}, u32[]{:S(2)}) collective-permute-start(bf16[384,768]{1,0:T(8,128)(2,1)S(1)} %get-tuple-element.259), channel_id=1, source_target_pairs={{0,8},{1,9},{2,10},{3,11},{4,12},{5,13},{6,14},{7,15},{8,0},{9,1},... | collective-permute-start | bytes 1769480 | tf_op jit(solution)/shard_map/ppermute | solution.py:1070
  170.7 27.2 %collective-permute-start.30 = (bf16[96,3840]{1,0:T(8,128)(2,1)}, bf16[96,3840]{1,0:T(8,128)(2,1)}, u32[]{:S(2)}, u32[]{:S(2)}) collective-permute-start(bf16[96,3840]{1,0:T(8,128)(2,1)} %get-tuple-element.256), channel_id=1, source_target_pairs={{0,2},{1,3},{2,0},{3,1},{4,6},{5,7},{6,4},{7,5},{8,10},{9,11},{10,... | collective-permute-start | bytes 2211848 | tf_op jit(solution)/shard_map/ppermute | solution.py:1070
  172.0 14.5 %copy-start.38 = (bf16[192,3840]{1,0:T(8,128)(2,1)S(1)}, bf16[192,3840]{1,0:T(8,128)(2,1)}, u32[]{:S(2)}) copy-start(bf16[192,3840]{1,0:T(8,128)(2,1)} %get-tuple-element.250) | copy-start | bytes 4423684
  197.9 3.5 %collective-permute-start.32 = (bf16[384,1280]{1,0:T(8,128)(2,1)}, bf16[384,1280]{1,0:T(8,128)(2,1)}, u32[]{:S(2)}, u32[]{:S(2)}) collective-permute-start(bf16[384,1280]{1,0:T(8,128)(2,1)} %get-tuple-element.149), channel_id=1, source_target_pairs={{0,1},{1,0},{2,3},{3,2},{4,5},{5,4},{6,7},{7,6},{8,9},{9,8},{10,11... | collective-permute-start | bytes 2949128 | tf_op jit(solution)/shard_map/ppermute | solution.py:1070
  197.9 19.2 %collective-permute-start.35 = (bf16[96,3840]{1,0:T(8,128)(2,1)}, bf16[96,3840]{1,0:T(8,128)(2,1)}, u32[]{:S(2)}, u32[]{:S(2)}) collective-permute-start(bf16[96,3840]{1,0:T(8,128)(2,1)} %add_convert_fusion.4), channel_id=1, source_target_pairs={{0,4},{1,5},{2,6},{3,7},{4,0},{5,1},{6,2},{7,3},{8,12},{9,13},{10,... | collective-permute-start | bytes 2211848 | tf_op jit(solution)/shard_map/ppermute | solution.py:1070
  199.8 41.2 %collective-permute-start.33 = (bf16[512,768]{1,0:T(8,128)(2,1)}, bf16[512,768]{1,0:T(8,128)(2,1)S(1)}, u32[]{:S(2)}, u32[]{:S(2)}) collective-permute-start(bf16[512,768]{1,0:T(8,128)(2,1)} %copy-done.24), channel_id=1, source_target_pairs={{0,16},{16,0},{1,17},{17,1},{2,18},{18,2},{3,19},{19,3},{4,20},{20... | collective-permute-start | bytes 2359304 | tf_op jit(solution)/shard_map/ppermute | solution.py:1073
  203.0 18.8 %collective-permute-start.34 = (bf16[192,1280]{1,0:T(8,128)(2,1)S(1)}, bf16[192,1280]{1,0:T(8,128)(2,1)S(1)}, u32[]{:S(2)}, u32[]{:S(2)}) collective-permute-start(bf16[192,1280]{1,0:T(8,128)(2,1)S(1)} %get-tuple-element.255), channel_id=1, source_target_pairs={{0,2},{1,3},{2,0},{3,1},{4,6},{5,7},{6,4},{7,5},{8,10},{9,11},{10,... | collective-permute-start | bytes 1474568 | tf_op jit(solution)/shard_map/ppermute | solution.py:1070
  206.7 13.5 %copy-start.39 = (bf16[384,768]{1,0:T(8,128)(2,1)S(1)}, bf16[384,768]{1,0:T(8,128)(2,1)}, u32[]{:S(2)}) copy-start(bf16[384,768]{1,0:T(8,128)(2,1)} %get-tuple-element.258) | copy-start | bytes 1769476
  206.7 13.5 %copy-start.45 = (bf16[384,768]{1,0:T(8,128)(2,1)S(1)}, bf16[384,768]{1,0:T(8,128)(2,1)}, u32[]{:S(2)}) copy-start(bf16[384,768]{1,0:T(8,128)(2,1)} %copy-done.44) | copy-start | bytes 1769476
  218.8 20.6 %collective-permute-start.40 = (bf16[48,3840]{1,0:T(8,128)(2,1)S(1)}, bf16[48,3840]{1,0:T(8,128)(2,1)S(1)}, u32[]{:S(2)}, u32[]{:S(2)}) collective-permute-start(bf16[48,3840]{1,0:T(8,128)(2,1)S(1)} %slice.284), channel_id=1, source_target_pairs={{0,8},{1,9},{2,10},{3,11},{4,12},{5,13},{6,14},{7,15},{8,0},{9,1},... | collective-permute-start | bytes 1105928 | tf_op jit(solution)/shard_map/ppermute | solution.py:1070
  220.3 8.4 %collective-permute-start.37 = (bf16[192,768]{1,0:T(8,128)(2,1)S(1)}, bf16[192,768]{1,0:T(8,128)(2,1)S(1)}, u32[]{:S(2)}, u32[]{:S(2)}) collective-permute-start(bf16[192,768]{1,0:T(8,128)(2,1)S(1)} %add_convert_fusion.11), channel_id=1, source_target_pairs={{0,2},{1,3},{2,0},{3,1},{4,6},{5,7},{6,4},{7,5},{8,10},{9,11},{10,... | collective-permute-start | bytes 884744 | tf_op jit(solution)/shard_map/ppermute | solution.py:1070
  222.0 11.3 %collective-permute-start.36 = (bf16[96,1280]{1,0:T(8,128)(2,1)S(1)}, bf16[96,1280]{1,0:T(8,128)(2,1)S(1)}, u32[]{:S(2)}, u32[]{:S(2)}) collective-permute-start(bf16[96,1280]{1,0:T(8,128)(2,1)S(1)} %get-tuple-element.262), channel_id=1, source_target_pairs={{0,4},{1,5},{2,6},{3,7},{4,0},{5,1},{6,2},{7,3},{8,12},{9,13},{10,... | collective-permute-start | bytes 737288 | tf_op jit(solution)/shard_map/ppermute | solution.py:1070
  228.8 15.5 %collective-permute-start.42 = (bf16[192,768]{1,0:T(8,128)(2,1)S(1)}, bf16[192,768]{1,0:T(8,128)(2,1)S(1)}, u32[]{:S(2)}, u32[]{:S(2)}) collective-permute-start(bf16[192,768]{1,0:T(8,128)(2,1)S(1)} %add_convert_fusion.9), channel_id=1, source_target_pairs={{0,16},{16,0},{1,17},{17,1},{2,18},{18,2},{3,19},{19,3},{4,20},{20... | collective-permute-start | bytes 884744 | tf_op jit(solution)/shard_map/ppermute | solution.py:1073
  233.3 9.8 %collective-permute-start.38 = (bf16[48,1280]{1,0:T(8,128)(2,1)S(1)}, bf16[48,1280]{1,0:T(8,128)(2,1)S(1)}, u32[]{:S(2)}, u32[]{:S(2)}) collective-permute-start(bf16[48,1280]{1,0:T(8,128)(2,1)S(1)} %add_convert_fusion.16), channel_id=1, source_target_pairs={{0,8},{1,9},{2,10},{3,11},{4,12},{5,13},{6,14},{7,15},{8,0},{9,1},... | collective-permute-start | bytes 368648 | tf_op jit(solution)/shard_map/ppermute | solution.py:1070
  239.5 15.7 %collective-permute-start.41 = (bf16[48,3840]{1,0:T(8,128)(2,1)S(1)}, bf16[48,3840]{1,0:T(8,128)(2,1)S(1)}, u32[]{:S(2)}, u32[]{:S(2)}) collective-permute-start(bf16[48,3840]{1,0:T(8,128)(2,1)S(1)} %fusion), channel_id=1, source_target_pairs={{0,16},{16,0},{1,17},{17,1},{2,18},{18,2},{3,19},{19,3},{4,20},{20... | collective-permute-start | bytes 1105928 | tf_op jit(solution)/shard_map/ppermute | solution.py:1073
  243.2 7.9 %collective-permute-start.39 = (bf16[48,1280]{1,0:T(8,128)(2,1)S(1)}, bf16[48,1280]{1,0:T(8,128)(2,1)S(1)}, u32[]{:S(2)}, u32[]{:S(2)}) collective-permute-start(bf16[48,1280]{1,0:T(8,128)(2,1)S(1)} %add_convert_fusion.14), channel_id=1, source_target_pairs={{0,16},{16,0},{1,17},{17,1},{2,18},{18,2},{3,19},{19,3},{4,20},{20... | collective-permute-start | bytes 368648 | tf_op jit(solution)/shard_map/ppermute | solution.py:1073
  (35 other events, 109.3 us)
where the time goes:
time: 260 us; the launch traced here: 257 us
  Pallas kernels  85.5 us (33%)
  waiting for transfers between devices  76.7 us (30%)
  starting transfers between devices  52.6 us (20%)
  local copies, waits for them, and re-layouts  22.8 us (9%)
  other arithmetic  17.4 us (7%)
    pallas_call x10, Pallas kernels, call(): pl.pallas_call(kernel, grid_spec=pltpu.PrefetchScalarGridSpec(num_scalar_...  85.5 us
    ppermute x34, waiting for transfers between devices, flip(): return lax.ppermute(array, 'fsdp', [(at, at ^ bit) for at in range(ring)])  59.7 us
    ppermute x34, starting transfers between devices, flip(): return lax.ppermute(array, 'fsdp', [(at, at ^ bit) for at in range(ring)])  40 us
    ppermute x9, waiting for transfers between devices, ctx_flip(): return lax.ppermute(array, 'ctx', [(0, 1), (1, 0)])  17 us
    ppermute x9, starting transfers between devices, ctx_flip(): return lax.ppermute(array, 'ctx', [(0, 1), (1, 0)])  12.6 us
    convert_element_type x11, other arithmetic, add(): return (left.astype(F32) + right.astype(F32)).astype(BF)  10.6 us
    unnamed x118, local copies, waits for them, and re-layouts  7.2 us
  transfers between devices with their start and end apart: 43, of which 21 were waited for; matrix products, arithmetic and copies ran while one was open for 11% of the time, Pallas kernels for 27%

commit v1 on v0

--- a/solution.py
+++ b/solution.py
@@ -664,7 +664,7 @@
             slope_ref[places, :] = slope.astype(BF)
             return carry
 
-        by_rows(rows, gelu_rows, 256)(0)
+        by_rows(rows, gelu_rows, 128)(0)
 
     outs = [(tile((rows, size), lambda i, info: (0, skip + i)), (rows, hidden), BF)] * 2
     scratch = [pltpu.VMEM((width, size), BF)]

time: 260 us -> 261 us (level)
  transfers between devices with their start and end apart: 43 -> 43, of which waited for: 21 -> 22; matrix products, arithmetic and copies ran while one was open for 11% -> 11% of each run, Pallas kernels for 27% -> 28%
where the time goes in v1:
time: 261 us; the launch traced here: 258 us
  Pallas kernels  86.6 us (33%)
  waiting for transfers between devices  77.8 us (30%)
  starting transfers between devices  51.2 us (20%)
  local copies, waits for them, and re-layouts  22.8 us (9%)
  other arithmetic  17.4 us (7%)
    pallas_call x10, Pallas kernels, call(): pl.pallas_call(kernel, grid_spec=pltpu.PrefetchScalarGridSpec(num_scalar_...  86.6 us
    ppermute x34, waiting for transfers between devices, flip(): return lax.ppermute(array, 'fsdp', [(at, at ^ bit) for at in range(ring)])  59.7 us
    ppermute x34, starting transfers between devices, flip(): return lax.ppermute(array, 'fsdp', [(at, at ^ bit) for at in range(ring)])  40.5 us
    ppermute x9, waiting for transfers between devices, ctx_flip(): return lax.ppermute(array, 'ctx', [(0, 1), (1, 0)])  18.1 us
    ppermute x9, starting transfers between devices, ctx_flip(): return lax.ppermute(array, 'ctx', [(0, 1), (1, 0)])  10.6 us
    convert_element_type x11, other arithmetic, add(): return (left.astype(F32) + right.astype(F32)).astype(BF)  10.6 us
    unnamed x118, local copies, waits for them, and re-layouts  7.2 us
  transfers between devices with their start and end apart: 43, of which 22 were waited for; matrix products, arithmetic and copies ran while one was open for 11% of the time, Pallas kernels for 28%

profile of v1, /device:TPU:0, one launch (start us, length us, event | category | flops | bytes accessed | tf_op | source)
XLA Modules:
  0.0 258.0 jit_solution(13379537270156849118)
XLA Ops:
  0.8 1.2 reshape.130
  2.7 4.1 %collective-permute-start.1 = (bf16[48,1280]{1,0:T(8,128)(2,1)S(1)}, bf16[48,1280]{1,0:T(8,128)(2,1)S(1)}, u32[]{:S(2)}, u32[]{:S(2)}) collective-permute-start(bf16[48,1280]{1,0:T(8,128)(2,1)S(1)} %pad_maximum_fusion.5), channel_id=1, source_target_pairs={{0,8},{1,9},{2,10},{3,11},{4,12},{5,13},{6,14},{7,15},{8,0},{9,1},... | collective-permute-start | bytes 368648 | tf_op jit(solution)/shard_map/ppermute | solution.py:1070
  7.6 1.5 collective-permute-start.6
  9.1 1.5 collective-permute-start
  11.4 1.2 collective-permute-done
  12.8 1.6 collective-permute-start.3
  14.4 2.6 %collective-permute-start.2 = (bf16[48,2304]{1,0:T(8,128)(2,1)S(1)}, bf16[48,2304]{1,0:T(8,128)(2,1)S(1)}, u32[]{:S(2)}, u32[]{:S(2)}) collective-permute-start(bf16[48,2304]{1,0:T(8,128)(2,1)S(1)} %pad_maximum_fusion.4), channel_id=1, source_target_pairs={{0,8},{1,9},{2,10},{3,11},{4,12},{5,13},{6,14},{7,15},{8,0},{9,1},... | collective-permute-start | bytes 663560 | tf_op jit(solution)/shard_map/ppermute | solution.py:1070
  17.0 6.8 %collective-permute-done.2 = bf16[48,2304]{1,0:T(8,128)(2,1)S(1)} collective-permute-done((bf16[48,2304]{1,0:T(8,128)(2,1)S(1)}, bf16[48,2304]{1,0:T(8,128)(2,1)S(1)}, u32[]{:S(2)}, u32[]{:S(2)}) %collective-permute-start.2) | collective-permute-done | bytes 221216 | tf_op jit(solution)/shard_map/ppermute | solution.py:1070
  24.8 3.2 %collective-permute-start.4 = (bf16[96,2304]{1,0:T(8,128)(2,1)S(1)}, bf16[96,2304]{1,0:T(8,128)(2,1)S(1)}, u32[]{:S(2)}, u32[]{:S(2)}) collective-permute-start(bf16[96,2304]{1,0:T(8,128)(2,1)S(1)} %constant_dynamic-update-slice_fusion), channel_id=1, source_target_pairs={{0,4},{1,5},{2,6},{3,7},{4,0},{5,1},{6,2},{7,3},{8,12},{9,13},{10,... | collective-permute-start | bytes 1327112 | tf_op jit(solution)/shard_map/ppermute | solution.py:1070
  28.3 2.3 collective-permute-start.5
  30.6 1.5 collective-permute-start.8
  32.1 8.9 %collective-permute-done.4 = bf16[96,2304]{1,0:T(8,128)(2,1)S(1)} collective-permute-done((bf16[96,2304]{1,0:T(8,128)(2,1)S(1)}, bf16[96,2304]{1,0:T(8,128)(2,1)S(1)}, u32[]{:S(2)}, u32[]{:S(2)}) %collective-permute-start.4) | collective-permute-done | bytes 442400 | tf_op jit(solution)/shard_map/ppermute | solution.py:1070
  41.0 1.6 collective-permute-start.12
  42.9 1.6 collective-permute-start.11
  44.5 1.1 pad_maximum_fusion
  45.6 2.1 collective-permute-start.17
  48.5 10.3 %shard_map.263 = (bf16[1024,768]{1,0:T(8,128)(2,1)S(1)}, bf16[512,256]{1,0:T(8,128)(2,1)S(1)}, bf16[512,256]{1,0:T(8,128)(2,1)S(1)}, f32[16,1024]{1,0:T(8,128)S(...) custom-call(s32[70]{0:T(128)S(1)} %concatenate.47.info, bf16[512,768]{1,0:T(8,128)(2,1)} %bitcast.31.rest_0_.rest_4_, ...), custom_call_target="tpu_custom_call" | custom-call | flops 345000000 | bytes 1 | tf_op jit(solution)/shard_map/pallas_call | solution.py:354
  58.9 1.6 collective-permute-start.13
  61.2 4.8 %shard_map.264 = (bf16[1024,384]{1,0:T(8,128)(2,1)S(1)}, bf16[512,128]{1,0:T(8,128)(2,1)S(1)}, bf16[512,128]{1,0:T(8,128)(2,1)}, f32[8,1024]{1,0:T(8,128)S(1)}) custom-call(s32[70]{0:T(128)S(1)} %concatenate.47.info, bf16[1024,768]{1,0:T(8,128)(2,1)S(1)} %get-tuple-element.97.rest_0_.low_ref, ...), custom_call_target="tpu_custom_call" | custom-call | flops 345000000 | bytes 1 | tf_op jit(solution)/shard_map/pallas_call | solution.py:354
  67.9 6.9 %collective-permute-done.17 = bf16[384,768]{1,0:T(8,128)(2,1)S(1)} collective-permute-done((bf16[384,768]{1,0:T(8,128)(2,1)S(1)}, bf16[384,768]{1,0:T(8,128)(2,1)S(1)}, u32[]{:S(2)}, u32[]{:S(2)}) %collective-permute-start.17) | collective-permute-done | bytes 589856 | tf_op jit(solution)/shard_map/ppermute | solution.py:1070
  76.1 1.5 collective-permute-start.18
  78.4 1.4 copy.110
  83.3 9.7 %shard_map.265 = (bf16[512,3072]{1,0:T(8,128)(2,1)S(1)}, bf16[512,3072]{1,0:T(8,128)(2,1)S(1)}, f32[512,768]{1,0:T(8,128)S(1)}, f32[512,128]{1,0:T(8,128)S(1)}, bf16[512,768]{1,0:T(8,128)(2,1)S(1)}) custom-call(s32[70]{0:T(128)S(1)} %concatenate.47.info, f32[1,3072]{1,0:T(1,128)S(1)} %reshape.135.ub_ref, ...), custom_call_target="tpu_custom_call" | custom-call | flops 345000000 | bytes 1 | tf_op jit(solution)/shard_map/pallas_call | solution.py:354
  93.6 1.8 collective-permute-done.19.rest_2_.rest_14_
  96.0 7.2 %shard_map.266 = (bf16[512,3072]{1,0:T(8,128)(2,1)S(1)}, bf16[512,3072]{1,0:T(8,128)(2,1)S(1)}) custom-call(s32[70]{0:T(128)S(1)} %concatenate.47.info, f32[1,3072]{1,0:T(1,128)S(1)} %reshape.135.ub_ref, bf16[192,1536]{1,0:T(8,128)(2,1)} %constant_dynamic-update-slice_fusion.4.rest_0_.rest_12_, ...), custom_call_target="tpu_custom_call", output_to_operand_aliasing={{0}: (7, {}), {1}: (8, {})} | custom-call | flops 345000000 | bytes 1 | tf_op jit(solution)/shard_map/pallas_call | solution.py:354
  104.0 2.5 collective-permute-done.22.rest_2_.rest_6_
  106.5 1.7 collective-permute-done.23.rest_3_.rest_7_
  108.2 15.0 %shard_map.267 = (f32[512,768]{1,0:T(8,128)}, f32[512,768]{1,0:T(8,128)S(1)}, bf16[512,768]{1,0:T(8,128)(2,1)S(1)}, f32[8,768]{1,0:T(8,128)S(1)}, bf16[1536,768]...) custom-call(s32[70]{0:T(128)S(1)} %concatenate.47.info, f32[16,768]{1,0:T(8,128)S(1)} %get-tuple-element.93.rest_5_.rest_10_.vec_ref, ...), custom_call_target="tpu_custom_call" | custom-call | flops 345000000 | bytes 1 | tf_op jit(solution)/shard_map/pallas_call | solution.py:354
  123.5 4.4 %collective-permute-done.24 = bf16[1536,768]{1,0:T(8,128)(2,1)S(1)} collective-permute-done((bf16[1536,768]{1,0:T(8,128)(2,1)S(1)}, bf16[1536,768]{1,0:T(8,128)(2,1)S(1)}, u32[]{:S(2)}, u32[]{:S(2)}) %collective-permute-start.24) | collective-permute-done | bytes 2359328 | tf_op jit(solution)/shard_map/ppermute | solution.py:1070
  127.9 1.7 add_convert_fusion.2
  130.4 1.8 collective-permute-start.25
  132.2 16.9 %shard_map.268 = (bf16[384,3840]{1,0:T(8,128)(2,1)S(1)}, bf16[384,3840]{1,0:T(8,128)(2,1)S(1)}, f32[1,3072]{1,0:T(1,128)S(1)}, f32[512,768]{1,0:T(8,128)S(1)}, b...) custom-call(s32[70]{0:T(128)S(1)} %concatenate.47.info, ...), custom_call_target="tpu_custom_call" | custom-call | flops 345000000 | bytes 1 | tf_op jit(solution)/shard_map/pallas_call | solution.py:354
  149.3 1.6 collective-permute-start.27
  151.3 9.5 %collective-permute-done.27.peer_ref = bf16[512,384]{1,0:T(8,128)(2,1)S(1)} collective-permute-done((bf16[512,384]{1,0:T(8,128)(2,1)S(1)}, bf16[512,384]{1,0:T(8,128)(2,1)S(1)}, u32[]{:S(2)}, u32[]{:S(2)}) %collective-permute-start.27) | collective-permute-done | bytes 393248 | tf_op jit(solution)/shard_map/ppermute | solution.py:1073
  160.8 1.8 add_convert_fusion
  162.7 1.3 fusion.1
  164.0 1.5 collective-permute-start.29
  166.9 2.7 %add_convert_fusion.5 = (bf16[384,768]{1,0:T(8,128)(2,1)}, bf16[384,768]{1,0:T(8,128)(2,1)S(1)}) fusion(bf16[384,768]{1,0:T(8,128)(2,1)S(1)} %copy-done.41, bf16[768,768]{1,0:T(8,128)(2,1)} %get-tuple-element.252, bf16[384,768]{1,0:T(8,128)(2,1)} %collective-permute-done.28), kind=kLoop, calls=%fused_computation.7 | loop fusion | flops 2359296 | bytes 3538944 | tf_op jit(solution)/shard_map/convert_element_type | solution.py:1174
  169.6 1.1 collective-permute-start.31
  170.7 1.3 collective-permute-start.30
  172.0 14.3 %shard_map.269 = (bf16[1024,1152]{1,0:T(8,128)(2,1)S(1)}, f32[24,128]{1,0:T(8,128)S(1)}) custom-call(s32[70]{0:T(128)S(1)} %concatenate.47.info, bf16[1024,768]{1,0:T(8,128)(2,1)S(1)} %copy-done.10, bf16[1024,384]{1,0:T(8,128)(2,1)S(1)} %copy-done.23, bf16[512,384]{1,0:T(8,128)(2,1)S(1)} %copy-done.26, bf16[512,384]{1,0:T(8,128)(2,1)S(1)} %copy-done.28, ...), custom_call_target="tpu_custom_call" | custom-call | flops 345000000 | bytes 1 | tf_op jit(solution)/shard_map/pallas_call | solution.py:354
  186.4 2.4 add_convert_fusion.4
  188.8 4.2 %shard_map.270 = (bf16[384,1280]{1,0:T(8,128)(2,1)S(1)}, bf16[384,1280]{1,0:T(8,128)(2,1)}) custom-call(s32[70]{0:T(128)S(1)} %concatenate.47.info, bf16[1024,768]{1,0:T(8,128)(2,1)S(1)} %copy-done.8, bf16[1024,1152]{1,0:T(8,128)(2,1)S(1)} %get-tuple-element.151.grad_ref, f32[24,128]{1,0:T(8,128)S(1)} %get-tuple-element.140.rest_0_, ...), custom_call_target="tpu_custom_call" | custom-call | flops 345000000 | bytes 1 | tf_op jit(solution)/shard_map/pallas_call | solution.py:354
  193.0 1.0 copy-done.19
  194.0 2.1 shard_map.271
  198.4 1.0 collective-permute-start.35
  199.4 1.2 slice.220
  201.6 1.6 add_convert_fusion.7
  203.2 1.6 collective-permute-start.34
  204.7 2.1 shard_map.272
  206.9 10.8 %collective-permute-done.35 = bf16[96,3840]{1,0:T(8,128)(2,1)} collective-permute-done((bf16[96,3840]{1,0:T(8,128)(2,1)}, bf16[96,3840]{1,0:T(8,128)(2,1)}, u32[]{:S(2)}, u32[]{:S(2)}) %collective-permute-start.35) | collective-permute-done | bytes 737312 | tf_op jit(solution)/shard_map/ppermute | solution.py:1070
  217.6 1.6 convert_add_fusion
  219.2 1.3 collective-permute-start.40
  220.6 1.2 collective-permute-start.37
  221.9 1.8 collective-permute-start.36
  223.7 5.3 %collective-permute-done.37 = bf16[192,768]{1,0:T(8,128)(2,1)S(1)} collective-permute-done((bf16[192,768]{1,0:T(8,128)(2,1)S(1)}, bf16[192,768]{1,0:T(8,128)(2,1)S(1)}, u32[]{:S(2)}, u32[]{:S(2)}) %collective-permute-start.37) | collective-permute-done | bytes 294944 | tf_op jit(solution)/shard_map/ppermute | solution.py:1070
  229.2 1.5 collective-permute-start.42
  230.7 2.9 %collective-permute-done.36 = bf16[96,1280]{1,0:T(8,128)(2,1)S(1)} collective-permute-done((bf16[96,1280]{1,0:T(8,128)(2,1)S(1)}, bf16[96,1280]{1,0:T(8,128)(2,1)S(1)}, u32[]{:S(2)}, u32[]{:S(2)}) %collective-permute-start.36) | collective-permute-done | bytes 245792 | tf_op jit(solution)/shard_map/ppermute | solution.py:1070
  233.6 3.3 %collective-permute-start.38 = (bf16[48,1280]{1,0:T(8,128)(2,1)S(1)}, bf16[48,1280]{1,0:T(8,128)(2,1)S(1)}, u32[]{:S(2)}, u32[]{:S(2)}) collective-permute-start(bf16[48,1280]{1,0:T(8,128)(2,1)S(1)} %add_convert_fusion.16), channel_id=1, source_target_pairs={{0,8},{1,9},{2,10},{3,11},{4,12},{5,13},{6,14},{7,15},{8,0},{9,1},... | collective-permute-start | bytes 368648 | tf_op jit(solution)/shard_map/ppermute | solution.py:1070
  236.9 4.7 %collective-permute-done.40 = bf16[48,3840]{1,0:T(8,128)(2,1)S(1)} collective-permute-done((bf16[48,3840]{1,0:T(8,128)(2,1)S(1)}, bf16[48,3840]{1,0:T(8,128)(2,1)S(1)}, u32[]{:S(2)}, u32[]{:S(2)}) %collective-permute-start.40) | collective-permute-done | bytes 368672 | tf_op jit(solution)/shard_map/ppermute | solution.py:1070
  241.7 1.3 add_bitcast_fusion
  243.6 1.5 collective-permute-start.39
  246.0 5.8 %collective-permute-done.39 = bf16[48,1280]{1,0:T(8,128)(2,1)S(1)} collective-permute-done((bf16[48,1280]{1,0:T(8,128)(2,1)S(1)}, bf16[48,1280]{1,0:T(8,128)(2,1)S(1)}, u32[]{:S(2)}, u32[]{:S(2)}) %collective-permute-start.39) | collective-permute-done | bytes 122912 | tf_op jit(solution)/shard_map/ppermute | solution.py:1073
  254.1 1.1 reshape.142
  (227 shorter events, 27.5 us)
Async XLA Ops:
  0.7 8.3 %copy-start.55 = (s32[1,2]{1,0:T(1,128)S(1)}, s32[1,2]{1,0:T(1,128)}, u32[]{:S(2)}) copy-start(s32[1,2]{1,0:T(1,128)} %param.18) | copy-start | bytes 28
  0.8 10.4 %copy-start.43 = (f32[48,3072]{1,0:T(8,128)S(1)}, f32[48,3072]{1,0:T(8,128)}, u32[]{:S(2)}) copy-start(f32[48,3072]{1,0:T(8,128)} %param.26) | copy-start | bytes 1769476
  2.2 8.9 %copy-start.46 = (f32[48,768]{1,0:T(8,128)S(1)}, f32[48,768]{1,0:T(8,128)}, u32[]{:S(2)}) copy-start(f32[48,768]{1,0:T(8,128)} %param.22) | copy-start | bytes 442372
  2.7 10.1 %collective-permute-start.1 = (bf16[48,1280]{1,0:T(8,128)(2,1)S(1)}, bf16[48,1280]{1,0:T(8,128)(2,1)S(1)}, u32[]{:S(2)}, u32[]{:S(2)}) collective-permute-start(bf16[48,1280]{1,0:T(8,128)(2,1)S(1)} %pad_maximum_fusion.5), channel_id=1, source_target_pairs={{0,8},{1,9},{2,10},{3,11},{4,12},{5,13},{6,14},{7,15},{8,0},{9,1},... | collective-permute-start | bytes 368648 | tf_op jit(solution)/shard_map/ppermute | solution.py:1070
  7.6 35.3 %collective-permute-start.6 = (bf16[192,768]{1,0:T(8,128)(2,1)}, bf16[192,768]{1,0:T(8,128)(2,1)}, u32[]{:S(2)}, u32[]{:S(2)}) collective-permute-start(bf16[192,768]{1,0:T(8,128)(2,1)} %convert_element_type.206), channel_id=1, source_target_pairs={{0,2},{1,3},{2,0},{3,1},{4,6},{5,7},{6,4},{7,5},{8,10},{9,11},{10,... | collective-permute-start | bytes 884744 | tf_op jit(solution)/shard_map/ppermute | solution.py:1070
  9.1 3.5 %collective-permute-start = (s32[1,2]{1,0:T(1,128)S(1)}, s32[1,2]{1,0:T(1,128)S(1)}, u32[]{:S(2)}, u32[]{:S(2)}) collective-permute-start(s32[1,2]{1,0:T(1,128)S(1)} %copy-done.55), channel_id=1, source_target_pairs={{0,16},{16,0},{1,17},{17,1},{2,18},{18,2},{3,19},{19,3},{4,20},{20... | collective-permute-start | bytes 32 | tf_op jit(solution)/shard_map/ppermute | solution.py:1073
  10.6 35.0 %collective-permute-start.7 = (bf16[512,768]{1,0:T(8,128)(2,1)}, bf16[512,768]{1,0:T(8,128)(2,1)}, u32[]{:S(2)}, u32[]{:S(2)}) collective-permute-start(bf16[512,768]{1,0:T(8,128)(2,1)} %bitcast.31.rest_0_.rest_4_), channel_id=1, source_target_pairs={{0,16},{16,0},{1,17},{17,1},{2,18},{18,2},{3,19},{19,3},{4,20},{20... | collective-permute-start | bytes 2359304 | tf_op jit(solution)/shard_map/ppermute | solution.py:1073
  12.8 11.9 %collective-permute-start.3 = (bf16[96,1280]{1,0:T(8,128)(2,1)S(1)}, bf16[96,1280]{1,0:T(8,128)(2,1)S(1)}, u32[]{:S(2)}, u32[]{:S(2)}) collective-permute-start(bf16[96,1280]{1,0:T(8,128)(2,1)S(1)} %pad_maximum_fusion.3), channel_id=1, source_target_pairs={{0,4},{1,5},{2,6},{3,7},{4,0},{5,1},{6,2},{7,3},{8,12},{9,13},{10,... | collective-permute-start | bytes 737288 | tf_op jit(solution)/shard_map/ppermute | solution.py:1070
  14.4 9.4 %collective-permute-start.2 = (bf16[48,2304]{1,0:T(8,128)(2,1)S(1)}, bf16[48,2304]{1,0:T(8,128)(2,1)S(1)}, u32[]{:S(2)}, u32[]{:S(2)}) collective-permute-start(bf16[48,2304]{1,0:T(8,128)(2,1)S(1)} %pad_maximum_fusion.4), channel_id=1, source_target_pairs={{0,8},{1,9},{2,10},{3,11},{4,12},{5,13},{6,14},{7,15},{8,0},{9,1},... | collective-permute-start | bytes 663560 | tf_op jit(solution)/shard_map/ppermute | solution.py:1070
  24.8 16.2 %collective-permute-start.4 = (bf16[96,2304]{1,0:T(8,128)(2,1)S(1)}, bf16[96,2304]{1,0:T(8,128)(2,1)S(1)}, u32[]{:S(2)}, u32[]{:S(2)}) collective-permute-start(bf16[96,2304]{1,0:T(8,128)(2,1)S(1)} %constant_dynamic-update-slice_fusion), channel_id=1, source_target_pairs={{0,4},{1,5},{2,6},{3,7},{4,0},{5,1},{6,2},{7,3},{8,12},{9,13},{10,... | collective-permute-start | bytes 1327112 | tf_op jit(solution)/shard_map/ppermute | solution.py:1070
  28.3 12.8 %collective-permute-start.5 = (bf16[48,1536]{1,0:T(8,128)(2,1)S(1)}, bf16[48,1536]{1,0:T(8,128)(2,1)S(1)}, u32[]{:S(2)}, u32[]{:S(2)}) collective-permute-start(bf16[48,1536]{1,0:T(8,128)(2,1)S(1)} %get-tuple-element.89), channel_id=1, source_target_pairs={{0,8},{1,9},{2,10},{3,11},{4,12},{5,13},{6,14},{7,15},{8,0},{9,1},... | collective-permute-start | bytes 442376 | tf_op jit(solution)/shard_map/ppermute | solution.py:1070
  30.6 12.0 %collective-permute-start.8 = (bf16[192,1280]{1,0:T(8,128)(2,1)S(1)}, bf16[192,1280]{1,0:T(8,128)(2,1)S(1)}, u32[]{:S(2)}, u32[]{:S(2)}) collective-permute-start(bf16[192,1280]{1,0:T(8,128)(2,1)S(1)} %pad_maximum_fusion.1.rest_3_.rest_7_.rest_1_.rest_0_), channel_id=1, source_target_pairs={{0,2},{1,3},{2,0},{3,1},{4,6},{5,7},{6,4},{7,5},{8,10},{9,11},{10,... | collective-permute-start | bytes 1474568 | tf_op jit(solution)/shard_map/ppermute | solution.py:1070
  32.1 16.4 %copy-start.37 = (bf16[1,768]{1,0:T(2,128)(2,1)S(1)}, bf16[1,768]{1,0:T(2,128)(2,1)}, u32[]{:S(2)}) copy-start(bf16[1,768]{1,0:T(2,128)(2,1)} %rest_5_.1) | copy-start | bytes 4612
  41.0 7.5 %collective-permute-start.9 = (bf16[192,1280]{1,0:T(8,128)(2,1)S(1)}, bf16[192,1280]{1,0:T(8,128)(2,1)S(1)}, u32[]{:S(2)}, u32[]{:S(2)}) collective-permute-start(bf16[192,1280]{1,0:T(8,128)(2,1)S(1)} %pad_maximum_fusion.1.rest_3_.rest_7_.rest_1_.rest_0_), channel_id=1, source_target_pairs={{0,1},{1,0},{2,3},{3,2},{4,5},{5,4},{6,7},{7,6},{8,9},{9,8},{10,11... | collective-permute-start | bytes 1474568 | tf_op jit(solution)/shard_map/ppermute | solution.py:1070
  41.0 25.9 %collective-permute-start.12 = (bf16[192,2304]{1,0:T(8,128)(2,1)S(1)}, bf16[192,2304]{1,0:T(8,128)(2,1)S(1)}, u32[]{:S(2)}, u32[]{:S(2)}) collective-permute-start(bf16[192,2304]{1,0:T(8,128)(2,1)S(1)} %constant_dynamic-update-slice_fusion.2.rest_0_.rest_11_.rest_8_.rest_16_), channel_id=1, source_target_pairs={{0,2},{1,3},{2,0},{3,1},{4,6},{5,7},{6,4},{7,5},{8,10},{9,11},{10,... | collective-permute-start | bytes 2654216 | tf_op jit(solution)/shard_map/ppermute | solution.py:1070
  42.6 5.9 %collective-permute-start.10 = (bf16[192,1280]{1,0:T(8,128)(2,1)S(1)}, bf16[192,1280]{1,0:T(8,128)(2,1)S(1)}, u32[]{:S(2)}, u32[]{:S(2)}) collective-permute-start(bf16[192,1280]{1,0:T(8,128)(2,1)S(1)} %collective-permute-done.8.rest_4_.rest_8_.rest_2_.rest_1_), channel_id=1, source_target_pairs={{0,1},{1,0},{2,3},{3,2},{4,5},{5,4},{6,7},{7,6},{8,9},{9,8},{10,11... | collective-permute-start | bytes 1474568 | tf_op jit(solution)/shard_map/ppermute | solution.py:1070
  42.9 17.6 %collective-permute-start.11 = (bf16[96,1536]{1,0:T(8,128)(2,1)S(1)}, bf16[96,1536]{1,0:T(8,128)(2,1)S(1)}, u32[]{:S(2)}, u32[]{:S(2)}) collective-permute-start(bf16[96,1536]{1,0:T(8,128)(2,1)S(1)} %pad_maximum_fusion.2), channel_id=1, source_target_pairs={{0,4},{1,5},{2,6},{3,7},{4,0},{5,1},{6,2},{7,3},{8,12},{9,13},{10,... | collective-permute-start | bytes 884744 | tf_op jit(solution)/shard_map/ppermute | solution.py:1070
  45.6 29.1 %collective-permute-start.17 = (bf16[384,768]{1,0:T(8,128)(2,1)S(1)}, bf16[384,768]{1,0:T(8,128)(2,1)S(1)}, u32[]{:S(2)}, u32[]{:S(2)}) collective-permute-start(bf16[384,768]{1,0:T(8,128)(2,1)S(1)} %pad_maximum_fusion), channel_id=1, source_target_pairs={{0,8},{1,9},{2,10},{3,11},{4,12},{5,13},{6,14},{7,15},{8,0},{9,1},... | collective-permute-start | bytes 1769480 | tf_op jit(solution)/shard_map/ppermute | solution.py:1070
  48.5 12.7 %copy-start.1 = (bf16[192,1280]{1,0:T(8,128)(2,1)}, bf16[192,1280]{1,0:T(8,128)(2,1)S(1)}, u32[]{:S(2)}) copy-start(bf16[192,1280]{1,0:T(8,128)(2,1)S(1)} %collective-permute-done.9.rest_5_.rest_9_.rest_3_.rest_2_) | copy-start | bytes 1474564
  48.5 12.7 %copy-start.4 = (bf16[192,1280]{1,0:T(8,128)(2,1)}, bf16[192,1280]{1,0:T(8,128)(2,1)S(1)}, u32[]{:S(2)}) copy-start(bf16[192,1280]{1,0:T(8,128)(2,1)S(1)} %collective-permute-done.10.rest_6_.rest_10_.rest_4_.rest_3_) | copy-start | bytes 1474564
  58.9 7.2 %copy-start.7 = (bf16[1024,768]{1,0:T(8,128)(2,1)}, bf16[1024,768]{1,0:T(8,128)(2,1)S(1)}, u32[]{:S(2)}) copy-start(bf16[1024,768]{1,0:T(8,128)(2,1)S(1)} %get-tuple-element.97.rest_0_.low_ref) | copy-start | bytes 4718596
  58.9 7.2 %copy-start.9 = (bf16[1024,768]{1,0:T(8,128)(2,1)}, bf16[1024,768]{1,0:T(8,128)(2,1)S(1)}, u32[]{:S(2)}) copy-start(bf16[1024,768]{1,0:T(8,128)(2,1)S(1)} %get-tuple-element.117.early_ref) | copy-start | bytes 4718596
  58.9 7.2 %copy-start.13 = (bf16[512,256]{1,0:T(8,128)(2,1)}, bf16[512,256]{1,0:T(8,128)(2,1)S(1)}, u32[]{:S(2)}) copy-start(bf16[512,256]{1,0:T(8,128)(2,1)S(1)} %get-tuple-element.104.rest_6_.rest_0_) | copy-start | bytes 786436
  58.9 7.2 %copy-start.29 = (f32[16,1024]{1,0:T(8,128)}, f32[16,1024]{1,0:T(8,128)S(1)}, u32[]{:S(2)}) copy-start(f32[16,1024]{1,0:T(8,128)S(1)} %get-tuple-element.135.lse0_ref) | copy-start | bytes 196612
  58.9 8.0 %collective-permute-start.13 = (bf16[512,256]{1,0:T(8,128)(2,1)S(1)}, bf16[512,256]{1,0:T(8,128)(2,1)S(1)}, u32[]{:S(2)}, u32[]{:S(2)}) collective-permute-start(bf16[512,256]{1,0:T(8,128)(2,1)S(1)} %get-tuple-element.94), channel_id=1, source_target_pairs={{0,16},{16,0},{1,17},{17,1},{2,18},{18,2},{3,19},{19,3},{4,20},{20... | collective-permute-start | bytes 786440 | tf_op jit(solution)/shard_map/ppermute | solution.py:1073
  66.1 8.7 %copy-start.22 = (bf16[1024,384]{1,0:T(8,128)(2,1)}, bf16[1024,384]{1,0:T(8,128)(2,1)S(1)}, u32[]{:S(2)}) copy-start(bf16[1024,384]{1,0:T(8,128)(2,1)S(1)} %get-tuple-element.118.late_ref) | copy-start | bytes 2359300
  66.1 9.2 %copy-start.31 = (f32[8,1024]{1,0:T(8,128)}, f32[8,1024]{1,0:T(8,128)S(1)}, u32[]{:S(2)}) copy-start(f32[8,1024]{1,0:T(8,128)S(1)} %get-tuple-element.136.lse1_ref) | copy-start | bytes 98308
  66.1 15.4 %collective-permute-start.15 = (bf16[192,2304]{1,0:T(8,128)(2,1)S(1)}, bf16[192,2304]{1,0:T(8,128)(2,1)}, u32[]{:S(2)}, u32[]{:S(2)}) collective-permute-start(bf16[192,2304]{1,0:T(8,128)(2,1)S(1)} %constant_dynamic-update-slice_fusion.2.rest_0_.rest_11_.rest_8_.rest_16_), channel_id=1, source_target_pairs={{0,1},{1,0},{2,3},{3,2},{4,5},{5,4},{6,7},{7,6},{8,9},{9,8},{10,11... | collective-permute-start | bytes 2654216 | tf_op jit(solution)/shard_map/ppermute | solution.py:1070
  66.9 14.5 %collective-permute-start.16 = (bf16[192,2304]{1,0:T(8,128)(2,1)S(1)}, bf16[192,2304]{1,0:T(8,128)(2,1)}, u32[]{:S(2)}, u32[]{:S(2)}) collective-permute-start(bf16[192,2304]{1,0:T(8,128)(2,1)S(1)} %collective-permute-done.12.rest_1_.rest_12_.rest_9_.rest_17_), channel_id=1, source_target_pairs={{0,1},{1,0},{2,3},{3,2},{4,5},{5,4},{6,7},{7,6},{8,9},{9,8},{10,11... | collective-permute-start | bytes 2654216 | tf_op jit(solution)/shard_map/ppermute | solution.py:1070
  74.7 18.3 %collective-permute-start.14 = (bf16[192,1536]{1,0:T(8,128)(2,1)}, bf16[192,1536]{1,0:T(8,128)(2,1)S(1)}, u32[]{:S(2)}, u32[]{:S(2)}) collective-permute-start(bf16[192,1536]{1,0:T(8,128)(2,1)} %constant_dynamic-update-slice_fusion.4.rest_0_.rest_12_), channel_id=1, source_target_pairs={{0,2},{1,3},{2,0},{3,1},{4,6},{5,7},{6,4},{7,5},{8,10},{9,11},{10,... | collective-permute-start | bytes 1769480 | tf_op jit(solution)/shard_map/ppermute | solution.py:1070
  76.1 27.3 %collective-permute-start.21 = (bf16[768,768]{1,0:T(8,128)(2,1)}, bf16[768,768]{1,0:T(8,128)(2,1)}, u32[]{:S(2)}, u32[]{:S(2)}) collective-permute-start(bf16[768,768]{1,0:T(8,128)(2,1)} %constant_dynamic-update-slice_fusion.6.rest_0_.rest_4_), channel_id=1, source_target_pairs={{0,4},{1,5},{2,6},{3,7},{4,0},{5,1},{6,2},{7,3},{8,12},{9,13},{10,... | collective-permute-start | bytes 3538952 | tf_op jit(solution)/shard_map/ppermute | solution.py:1070
  76.1 5.3 %collective-permute-start.18 = (bf16[512,128]{1,0:T(8,128)(2,1)}, bf16[512,128]{1,0:T(8,128)(2,1)}, u32[]{:S(2)}, u32[]{:S(2)}) collective-permute-start(bf16[512,128]{1,0:T(8,128)(2,1)} %get-tuple-element.98), channel_id=1, source_target_pairs={{0,16},{16,0},{1,17},{17,1},{2,18},{18,2},{3,19},{19,3},{4,20},{20... | collective-permute-start | bytes 393224 | tf_op jit(solution)/shard_map/ppermute | solution.py:1073
  93.0 2.3 collective-permute-start.19
  93.1 2.8 %collective-permute-start.20 = (bf16[192,1536]{1,0:T(8,128)(2,1)S(1)}, bf16[192,1536]{1,0:T(8,128)(2,1)S(1)}, u32[]{:S(2)}, u32[]{:S(2)}) collective-permute-start(bf16[192,1536]{1,0:T(8,128)(2,1)S(1)} %collective-permute-done.14.rest_1_.rest_13_), channel_id=1, source_target_pairs={{0,1},{1,0},{2,3},{3,2},{4,5},{5,4},{6,7},{7,6},{8,9},{9,8},{10,11... | collective-permute-start | bytes 1769480 | tf_op jit(solution)/shard_map/ppermute | solution.py:1070
  96.0 12.3 %copy-start.21 = (bf16[1,512,768]{2,1,0:T(8,128)(2,1)S(1)}, bf16[1,512,768]{2,1,0:T(8,128)(2,1)}, u32[]{:S(2)}) copy-start(bf16[1,512,768]{2,1,0:T(8,128)(2,1)} %param.19) | copy-start | bytes 2359300
  103.1 20.1 %copy-start = (bf16[512,3072]{1,0:T(8,128)(2,1)}, bf16[512,3072]{1,0:T(8,128)(2,1)S(1)}, u32[]{:S(2)}) copy-start(bf16[512,3072]{1,0:T(8,128)(2,1)S(1)} %get-tuple-element.123.slope_ref) | copy-start | bytes 9437188
  103.5 3.1 %collective-permute-start.22 = (bf16[768,768]{1,0:T(8,128)(2,1)}, bf16[768,768]{1,0:T(8,128)(2,1)S(1)}, u32[]{:S(2)}, u32[]{:S(2)}) collective-permute-start(bf16[768,768]{1,0:T(8,128)(2,1)} %constant_dynamic-update-slice_fusion.6.rest_0_.rest_4_), channel_id=1, source_target_pairs={{0,1},{1,0},{2,3},{3,2},{4,5},{5,4},{6,7},{7,6},{8,9},{9,8},{10,11... | collective-permute-start | bytes 3538952 | tf_op jit(solution)/shard_map/ppermute | solution.py:1070
  103.5 4.7 %collective-permute-start.23 = (bf16[768,768]{1,0:T(8,128)(2,1)}, bf16[768,768]{1,0:T(8,128)(2,1)S(1)}, u32[]{:S(2)}, u32[]{:S(2)}) collective-permute-start(bf16[768,768]{1,0:T(8,128)(2,1)} %collective-permute-done.21.rest_1_.rest_5_), channel_id=1, source_target_pairs={{0,1},{1,0},{2,3},{3,2},{4,5},{5,4},{6,7},{7,6},{8,9},{9,8},{10,11... | collective-permute-start | bytes 3538952 | tf_op jit(solution)/shard_map/ppermute | solution.py:1070
  123.3 4.6 %collective-permute-start.24 = (bf16[1536,768]{1,0:T(8,128)(2,1)S(1)}, bf16[1536,768]{1,0:T(8,128)(2,1)S(1)}, u32[]{:S(2)}, u32[]{:S(2)}) collective-permute-start(bf16[1536,768]{1,0:T(8,128)(2,1)S(1)} %get-tuple-element.121), channel_id=1, source_target_pairs={{0,1},{1,0},{2,3},{3,2},{4,5},{5,4},{6,7},{7,6},{8,9},{9,8},{10,11... | collective-permute-start | bytes 7077896 | tf_op jit(solution)/shard_map/ppermute | solution.py:1070
  130.4 18.7 %collective-permute-start.25 = (bf16[384,768]{1,0:T(8,128)(2,1)S(1)}, bf16[384,768]{1,0:T(8,128)(2,1)S(1)}, u32[]{:S(2)}, u32[]{:S(2)}) collective-permute-start(bf16[384,768]{1,0:T(8,128)(2,1)S(1)} %get-tuple-element.261), channel_id=1, source_target_pairs={{0,4},{1,5},{2,6},{3,7},{4,0},{5,1},{6,2},{7,3},{8,12},{9,13},{10,... | collective-permute-start | bytes 1769480 | tf_op jit(solution)/shard_map/ppermute | solution.py:1070
  149.1 13.5 %copy-start.11 = (f32[512,768]{1,0:T(8,128)}, f32[512,768]{1,0:T(8,128)S(1)}, u32[]{:S(2)}) copy-start(f32[512,768]{1,0:T(8,128)S(1)} %get-tuple-element.152.rest_4_) | copy-start | bytes 4718596
  149.1 13.5 %copy-start.25 = (bf16[512,384]{1,0:T(8,128)(2,1)}, bf16[512,384]{1,0:T(8,128)(2,1)S(1)}, u32[]{:S(2)}) copy-start(bf16[512,384]{1,0:T(8,128)(2,1)S(1)} %get-tuple-element.134.own_ref) | copy-start | bytes 1179652
  149.1 13.5 %copy-start.35 = (f32[8,768]{1,0:T(8,128)}, f32[8,768]{1,0:T(8,128)S(1)}, u32[]{:S(2)}) copy-start(f32[8,768]{1,0:T(8,128)S(1)} %get-tuple-element.141.rest_1_) | copy-start | bytes 73732
  149.2 13.5 %copy-start.40 = (bf16[384,768]{1,0:T(8,128)(2,1)}, bf16[384,768]{1,0:T(8,128)(2,1)S(1)}, u32[]{:S(2)}) copy-start(bf16[384,768]{1,0:T(8,128)(2,1)S(1)} %collective-permute-done.25) | copy-start | bytes 1769476
  149.2 11.6 %collective-permute-start.26 = (bf16[384,3840]{1,0:T(8,128)(2,1)S(1)}, bf16[384,3840]{1,0:T(8,128)(2,1)S(1)}, u32[]{:S(2)}, u32[]{:S(2)}) collective-permute-start(bf16[384,3840]{1,0:T(8,128)(2,1)S(1)} %get-tuple-element.130), channel_id=1, source_target_pairs={{0,1},{1,0},{2,3},{3,2},{4,5},{5,4},{6,7},{7,6},{8,9},{9,8},{10,11... | collective-permute-start | bytes 8847368 | tf_op jit(solution)/shard_map/ppermute | solution.py:1070
  149.3 11.5 %collective-permute-start.27 = (bf16[512,384]{1,0:T(8,128)(2,1)S(1)}, bf16[512,384]{1,0:T(8,128)(2,1)S(1)}, u32[]{:S(2)}, u32[]{:S(2)}) collective-permute-start(bf16[512,384]{1,0:T(8,128)(2,1)S(1)} %get-tuple-element.131), channel_id=1, source_target_pairs={{0,16},{16,0},{1,17},{17,1},{2,18},{18,2},{3,19},{19,3},{4,20},{20... | collective-permute-start | bytes 1179656 | tf_op jit(solution)/shard_map/ppermute | solution.py:1073
  150.8 16.1 %collective-permute-start.28 = (bf16[384,768]{1,0:T(8,128)(2,1)}, bf16[384,768]{1,0:T(8,128)(2,1)}, u32[]{:S(2)}, u32[]{:S(2)}) collective-permute-start(bf16[384,768]{1,0:T(8,128)(2,1)} %get-tuple-element.260), channel_id=1, source_target_pairs={{0,4},{1,5},{2,6},{3,7},{4,0},{5,1},{6,2},{7,3},{8,12},{9,13},{10,... | collective-permute-start | bytes 1769480 | tf_op jit(solution)/shard_map/ppermute | solution.py:1070
  164.0 22.4 %collective-permute-start.29 = (bf16[96,3840]{1,0:T(8,128)(2,1)}, bf16[96,3840]{1,0:T(8,128)(2,1)}, u32[]{:S(2)}, u32[]{:S(2)}) collective-permute-start(bf16[96,3840]{1,0:T(8,128)(2,1)} %get-tuple-element.257), channel_id=1, source_target_pairs={{0,2},{1,3},{2,0},{3,1},{4,6},{5,7},{6,4},{7,5},{8,10},{9,11},{10,... | collective-permute-start | bytes 2211848 | tf_op jit(solution)/shard_map/ppermute | solution.py:1070
  169.6 27.9 %collective-permute-start.31 = (bf16[384,768]{1,0:T(8,128)(2,1)S(1)}, bf16[384,768]{1,0:T(8,128)(2,1)S(1)}, u32[]{:S(2)}, u32[]{:S(2)}) collective-permute-start(bf16[384,768]{1,0:T(8,128)(2,1)S(1)} %get-tuple-element.259), channel_id=1, source_target_pairs={{0,8},{1,9},{2,10},{3,11},{4,12},{5,13},{6,14},{7,15},{8,0},{9,1},... | collective-permute-start | bytes 1769480 | tf_op jit(solution)/shard_map/ppermute | solution.py:1070
  170.7 27.7 %collective-permute-start.30 = (bf16[96,3840]{1,0:T(8,128)(2,1)}, bf16[96,3840]{1,0:T(8,128)(2,1)}, u32[]{:S(2)}, u32[]{:S(2)}) collective-permute-start(bf16[96,3840]{1,0:T(8,128)(2,1)} %get-tuple-element.256), channel_id=1, source_target_pairs={{0,2},{1,3},{2,0},{3,1},{4,6},{5,7},{6,4},{7,5},{8,10},{9,11},{10,... | collective-permute-start | bytes 2211848 | tf_op jit(solution)/shard_map/ppermute | solution.py:1070
  172.0 14.4 %copy-start.38 = (bf16[192,3840]{1,0:T(8,128)(2,1)S(1)}, bf16[192,3840]{1,0:T(8,128)(2,1)}, u32[]{:S(2)}) copy-start(bf16[192,3840]{1,0:T(8,128)(2,1)} %get-tuple-element.250) | copy-start | bytes 4423684
  198.4 3.2 %collective-permute-start.32 = (bf16[384,1280]{1,0:T(8,128)(2,1)}, bf16[384,1280]{1,0:T(8,128)(2,1)}, u32[]{:S(2)}, u32[]{:S(2)}) collective-permute-start(bf16[384,1280]{1,0:T(8,128)(2,1)} %get-tuple-element.149), channel_id=1, source_target_pairs={{0,1},{1,0},{2,3},{3,2},{4,5},{5,4},{6,7},{7,6},{8,9},{9,8},{10,11... | collective-permute-start | bytes 2949128 | tf_op jit(solution)/shard_map/ppermute | solution.py:1070
  198.4 19.2 %collective-permute-start.35 = (bf16[96,3840]{1,0:T(8,128)(2,1)}, bf16[96,3840]{1,0:T(8,128)(2,1)}, u32[]{:S(2)}, u32[]{:S(2)}) collective-permute-start(bf16[96,3840]{1,0:T(8,128)(2,1)} %add_convert_fusion.4), channel_id=1, source_target_pairs={{0,4},{1,5},{2,6},{3,7},{4,0},{5,1},{6,2},{7,3},{8,12},{9,13},{10,... | collective-permute-start | bytes 2211848 | tf_op jit(solution)/shard_map/ppermute | solution.py:1070
  200.7 41.0 %collective-permute-start.33 = (bf16[512,768]{1,0:T(8,128)(2,1)}, bf16[512,768]{1,0:T(8,128)(2,1)S(1)}, u32[]{:S(2)}, u32[]{:S(2)}) collective-permute-start(bf16[512,768]{1,0:T(8,128)(2,1)} %copy-done.24), channel_id=1, source_target_pairs={{0,16},{16,0},{1,17},{17,1},{2,18},{18,2},{3,19},{19,3},{4,20},{20... | collective-permute-start | bytes 2359304 | tf_op jit(solution)/shard_map/ppermute | solution.py:1073
  203.2 18.6 %collective-permute-start.34 = (bf16[192,1280]{1,0:T(8,128)(2,1)S(1)}, bf16[192,1280]{1,0:T(8,128)(2,1)S(1)}, u32[]{:S(2)}, u32[]{:S(2)}) collective-permute-start(bf16[192,1280]{1,0:T(8,128)(2,1)S(1)} %get-tuple-element.255), channel_id=1, source_target_pairs={{0,2},{1,3},{2,0},{3,1},{4,6},{5,7},{6,4},{7,5},{8,10},{9,11},{10,... | collective-permute-start | bytes 1474568 | tf_op jit(solution)/shard_map/ppermute | solution.py:1070
  206.8 13.7 %copy-start.39 = (bf16[384,768]{1,0:T(8,128)(2,1)S(1)}, bf16[384,768]{1,0:T(8,128)(2,1)}, u32[]{:S(2)}) copy-start(bf16[384,768]{1,0:T(8,128)(2,1)} %get-tuple-element.258) | copy-start | bytes 1769476
  206.8 13.7 %copy-start.45 = (bf16[384,768]{1,0:T(8,128)(2,1)S(1)}, bf16[384,768]{1,0:T(8,128)(2,1)}, u32[]{:S(2)}) copy-start(bf16[384,768]{1,0:T(8,128)(2,1)} %copy-done.44) | copy-start | bytes 1769476
  219.2 22.3 %collective-permute-start.40 = (bf16[48,3840]{1,0:T(8,128)(2,1)S(1)}, bf16[48,3840]{1,0:T(8,128)(2,1)S(1)}, u32[]{:S(2)}, u32[]{:S(2)}) collective-permute-start(bf16[48,3840]{1,0:T(8,128)(2,1)S(1)} %slice.284), channel_id=1, source_target_pairs={{0,8},{1,9},{2,10},{3,11},{4,12},{5,13},{6,14},{7,15},{8,0},{9,1},... | collective-permute-start | bytes 1105928 | tf_op jit(solution)/shard_map/ppermute | solution.py:1070
  220.6 8.4 %collective-permute-start.37 = (bf16[192,768]{1,0:T(8,128)(2,1)S(1)}, bf16[192,768]{1,0:T(8,128)(2,1)S(1)}, u32[]{:S(2)}, u32[]{:S(2)}) collective-permute-start(bf16[192,768]{1,0:T(8,128)(2,1)S(1)} %add_convert_fusion.11), channel_id=1, source_target_pairs={{0,2},{1,3},{2,0},{3,1},{4,6},{5,7},{6,4},{7,5},{8,10},{9,11},{10,... | collective-permute-start | bytes 884744 | tf_op jit(solution)/shard_map/ppermute | solution.py:1070
  221.9 11.7 %collective-permute-start.36 = (bf16[96,1280]{1,0:T(8,128)(2,1)S(1)}, bf16[96,1280]{1,0:T(8,128)(2,1)S(1)}, u32[]{:S(2)}, u32[]{:S(2)}) collective-permute-start(bf16[96,1280]{1,0:T(8,128)(2,1)S(1)} %get-tuple-element.262), channel_id=1, source_target_pairs={{0,4},{1,5},{2,6},{3,7},{4,0},{5,1},{6,2},{7,3},{8,12},{9,13},{10,... | collective-permute-start | bytes 737288 | tf_op jit(solution)/shard_map/ppermute | solution.py:1070
  229.2 16.0 %collective-permute-start.42 = (bf16[192,768]{1,0:T(8,128)(2,1)S(1)}, bf16[192,768]{1,0:T(8,128)(2,1)S(1)}, u32[]{:S(2)}, u32[]{:S(2)}) collective-permute-start(bf16[192,768]{1,0:T(8,128)(2,1)S(1)} %add_convert_fusion.9), channel_id=1, source_target_pairs={{0,16},{16,0},{1,17},{17,1},{2,18},{18,2},{3,19},{19,3},{4,20},{20... | collective-permute-start | bytes 884744 | tf_op jit(solution)/shard_map/ppermute | solution.py:1073
  233.6 10.0 %collective-permute-start.38 = (bf16[48,1280]{1,0:T(8,128)(2,1)S(1)}, bf16[48,1280]{1,0:T(8,128)(2,1)S(1)}, u32[]{:S(2)}, u32[]{:S(2)}) collective-permute-start(bf16[48,1280]{1,0:T(8,128)(2,1)S(1)} %add_convert_fusion.16), channel_id=1, source_target_pairs={{0,8},{1,9},{2,10},{3,11},{4,12},{5,13},{6,14},{7,15},{8,0},{9,1},... | collective-permute-start | bytes 368648 | tf_op jit(solution)/shard_map/ppermute | solution.py:1070
  241.7 14.3 %collective-permute-start.41 = (bf16[48,3840]{1,0:T(8,128)(2,1)S(1)}, bf16[48,3840]{1,0:T(8,128)(2,1)S(1)}, u32[]{:S(2)}, u32[]{:S(2)}) collective-permute-start(bf16[48,3840]{1,0:T(8,128)(2,1)S(1)} %fusion), channel_id=1, source_target_pairs={{0,16},{16,0},{1,17},{17,1},{2,18},{18,2},{3,19},{19,3},{4,20},{20... | collective-permute-start | bytes 1105928 | tf_op jit(solution)/shard_map/ppermute | solution.py:1073
  243.6 8.2 %collective-permute-start.39 = (bf16[48,1280]{1,0:T(8,128)(2,1)S(1)}, bf16[48,1280]{1,0:T(8,128)(2,1)S(1)}, u32[]{:S(2)}, u32[]{:S(2)}) collective-permute-start(bf16[48,1280]{1,0:T(8,128)(2,1)S(1)} %add_convert_fusion.14), channel_id=1, source_target_pairs={{0,16},{16,0},{1,17},{17,1},{2,18},{18,2},{3,19},{19,3},{4,20},{20... | collective-permute-start | bytes 368648 | tf_op jit(solution)/shard_map/ppermute | solution.py:1073
  (35 other events, 103.8 us)
